TPU v7x, 32 devices: a whole 2x2x4 slice. The times are simulated.
32 devices in a mesh: dp: 16 (over z, y, x), tensor: 2 (over core).
Axes of the slice: x: 2, y: 2, z: 4, core: 2. Of those that a mesh axis runs over, the one named last changes fastest.
Arguments:
- inputs: bfloat16 [16, 1024, 768], P('dp', 'tensor'), may hold values from -6 to 6
- cotangent: bfloat16 [16, 1024, 768], P('dp', 'tensor'), may hold values from -6 to 6
- lengths: int32 [16], P('dp'), may hold values from 576 to 1024, as said below
- query_key: bfloat16 [768, 1536], P(('dp', 'tensor')), may hold values from -0.21875 to 0.21875
- value_proj: bfloat16 [768, 768], P(('dp', 'tensor')), may hold values from -0.375 to 0.375
- output_proj: bfloat16 [768, 768], P(('dp', 'tensor')), may hold values from -0.375 to 0.375
- hidden_in: bfloat16 [768, 3072], P('dp', 'tensor'), may hold values from -2 to 2
- hidden_out: bfloat16 [3072, 768], P('tensor', 'dp'), may hold values from -2 to 2
- first_gain: bfloat16 [768], P(('dp', 'tensor')), may hold values from 0.25 to 1.75
- second_gain: bfloat16 [768], P(('dp', 'tensor')), may hold values from 0.25 to 1.75
- third_gain: bfloat16 [768], P(('dp', 'tensor')), may hold values from 0.25 to 1.75
- fourth_gain: bfloat16 [3072], P('tensor'), may hold values from 0.25 to 1.75
Outputs:
- outputs: bfloat16 [16, 1024, 768], P('dp', 'tensor')
- inputs_grad: bfloat16 [16, 1024, 768], P('dp', 'tensor')
- query_key_grad: float32 [768, 1536], P(('dp', 'tensor'))
- value_proj_grad: float32 [768, 768], P(('dp', 'tensor'))
- output_proj_grad: float32 [768, 768], P(('dp', 'tensor'))
- hidden_in_grad: float32 [768, 3072], P('dp', 'tensor')
- hidden_out_grad: float32 [3072, 768], P('tensor', 'dp')
- first_gain_grad: float32 [768], P(('dp', 'tensor'))
- second_gain_grad: float32 [768], P(('dp', 'tensor'))
- third_gain_grad: float32 [768], P(('dp', 'tensor'))
- fourth_gain_grad: float32 [3072], P('tensor')
Inputs may be any that keep to these rules, and one draw needn't show every extreme that they name: `lengths`: shorter sequences are more common; at least one sequence has exactly 1024 tokens.
All inputs are finite; a program needn't handle non-finite values.
Results may differ from a plain program's by a relative error of at most 0.019.
Values may be sent and summed in bfloat16 or wider, within the bound.
No kernel may reach another device: no remote copies, remote signals or barrier semaphores. Data moves between devices by JAX's collectives and lax.ppermute only.
A program may use at most 128 MiB of HBM per device.

v0:
```python
import jax
import jax.numpy as jnp
from jax import lax
from jax.experimental import pallas as pl
from jax.experimental.pallas import tpu as pltpu
from jax.sharding import Mesh
from jax.sharding import PartitionSpec as P

HEAD_DIM = 64
PAIR = 2 * HEAD_DIM
EPSILON = 1e-05
MASKED = -1000000000.0
F32 = jnp.float32
BF16 = jnp.bfloat16
VMEM_LIMIT = 60 * 1024 * 1024
TILE = 256
EXTRA = 16
COST_SCALE = 0.05
COSTS = {
    "project": 8,
    "attend": 15,
    "join": 5,
    "ffn_in": 10,
    "ffn_out": 10,
    "ffn_back": 14,
    "join_back": 7,
    "attend_back": 20,
    "project_grads": 11,
    "project_back": 7,
}


def mm(former, latter):
    return jnp.dot(former, latter, preferred_element_type=F32)


def mm_tail(former, latter):
    return lax.dot_general(former, latter, (((1,), (1,)), ((), ())), preferred_element_type=F32)


def mm_lead(former, latter):
    return lax.dot_general(former, latter, (((0,), (0,)), ((), ())), preferred_element_type=F32)


def call(body, name, out_shape, grid, in_specs, out_specs, scratch=(), aliases=None):
    return pl.pallas_call(
        body,
        name=name,
        out_shape=out_shape,
        grid_spec=pltpu.PrefetchScalarGridSpec(
            num_scalar_prefetch=1,
            grid=grid,
            in_specs=in_specs,
            out_specs=out_specs,
            scratch_shapes=list(scratch),
        ),
        input_output_aliases=aliases or {},
        compiler_params=pltpu.CompilerParams(vmem_limit_bytes=VMEM_LIMIT),
        cost_estimate=pl.CostEstimate(
            flops=1, bytes_accessed=int(COST_SCALE * COSTS[name] * 3690000), transcendentals=0
        ),
    )


def shaped(shape, kind):
    return jax.ShapeDtypeStruct(shape, kind)


def whole(shape):
    return pl.BlockSpec(shape, lambda i, s: (0,) * len(shape), pipeline_mode=pl.Buffered(1))


def rows_of(shape):
    return pl.BlockSpec(shape, lambda i, s: (i, 0))


def norm_stats(series):
    center = jnp.mean(series, -1, keepdims=True)
    spread = jnp.mean(series * series, -1, keepdims=True) - center * center
    inverse = lax.rsqrt(spread + EPSILON)
    return (series - center) * inverse, inverse


def norm_back(grad, gain, hat, inverse):
    scaled = grad * gain
    first = jnp.mean(scaled, -1, keepdims=True)
    second = jnp.mean(scaled * hat, -1, keepdims=True)
    return inverse * (scaled - first - hat * second)


def put_blocks(s_ref, pieces, places, target, column, width):
    at = 0
    for piece in pieces:
        depth = piece.shape[1]
        for block in range(piece.shape[0]):
            row = (s_ref[0] ^ places[at]) * depth
            if depth % 16 == 0:
                row = pl.multiple_of(row, 16)
            target[pl.ds(row, depth), pl.ds(column, width)] = piece[block, :, 0:width]
            at += 1


def put_rows(s_ref, mine, other, places, target, column, folds):
    near = s_ref[1] == 0
    own = mine.shape[1] // folds
    width = mine.shape[2]
    for block in range(mine.shape[0]):
        row = pl.multiple_of((s_ref[0] ^ places[block]) * (2 * own), 16)
        one, two = mine[block].astype(F32), other[block].astype(F32)
        upper, lower = jnp.where(near, one, two), jnp.where(near, two, one)
        for at in range(folds):
            rows = slice(at * own, (at + 1) * own)
            target[pl.ds(row, 2 * own), column + at * width : column + (at + 1) * width] = jnp.concatenate(
                [upper[rows], lower[rows]], 0
            ).astype(BF16)


def project(inputs, parts, places, scalars):
    rows, width = inputs.shape
    tile = min(TILE, rows)
    flat = [piece for part in parts for piece in part]
    cuts = [part[0].shape[2] for part in parts]
    columns = sum(cuts)

    def body(s_ref, x_ref, *refs):
        pieces, (q_ref, kv_ref, n_ref, w_ref, g_ref, full) = refs[: len(flat)], refs[len(flat) :]

        @pl.when(pl.program_id(0) == 0)
        def _():
            at = 0
            for k, part in enumerate(parts):
                column = sum(cuts[:k])
                if len(part) == 2:
                    put_rows(s_ref, pieces[at], pieces[at + 1], places[k], full, column, 1)
                else:
                    put_blocks(s_ref, pieces[at : at + 1], places[k], full, column, cuts[k])
                at += len(part)
            w_ref[...] = full[:, 0 : 3 * width]
            g_ref[...] = jnp.transpose(full[:, 3 * width : 3 * width + 128].astype(F32))[0:8]

        hat, _ = norm_stats(x_ref[...].astype(F32))
        low = (hat * g_ref[0:1, :]).astype(BF16)
        n_ref[...] = low
        q_ref[...] = mm(low, full[:, 0:width]).astype(BF16)
        for which in range(2):
            part = mm(low, full[:, (1 + which) * width : (2 + which) * width]).astype(BF16)
            for pair in range(width // PAIR):
                at = (2 * pair + which) * PAIR
                kv_ref[:, at : at + PAIR] = part[:, pair * PAIR : (pair + 1) * PAIR]

    spec = rows_of((tile, width))
    return call(
        body,
        "project",
        (
            shaped((rows, width), BF16),
            shaped((rows, 2 * width), BF16),
            shaped((rows, width), BF16),
            shaped((width, 3 * width), BF16),
            shaped((8, width), F32),
        ),
        (rows // tile,),
        [spec] + [whole(p.shape) for p in flat],
        (spec, rows_of((tile, 2 * width)), spec, whole((width, 3 * width)), whole((8, width))),
        scratch=[pltpu.VMEM((width, columns), BF16)],
    )(scalars, inputs, *flat)


def lane_of(head):
    lanes = lax.broadcasted_iota(jnp.int32, (1, PAIR), 1)
    return (lanes >= head * HEAD_DIM) & (lanes < (head + 1) * HEAD_DIM)


def attend(queries, near, far_side, scalars):
    rows, width = queries.shape
    tile = min(TILE, rows)
    pairs = width // PAIR

    def body(s_ref, q_ref, kv_ref, fkv_ref, o_ref, l_ref):
        offset = s_ref[1] * rows
        length = s_ref[2]

        def run(far):
            query = q_ref[...] * jnp.asarray(0.125, BF16)
            for t in range(rows // tile):
                end = (t + 1) * tile
                place = lax.broadcasted_iota(jnp.int32, (tile, end), 0) + t * tile
                key_at = lax.broadcasted_iota(jnp.int32, (tile, end), 1)
                allowed = (key_at <= place) & (key_at + offset < length)
                sums = []
                logs = []
                for head in range(2):
                    mine = jnp.where(
                        lane_of(head), query[t * tile : end], jnp.zeros((), BF16)
                    )
                    scores = jnp.where(allowed, mm_tail(mine, kv_ref[0:end, 0:PAIR]), MASKED)
                    highest = jnp.max(scores, -1, keepdims=True)
                    if far:
                        beyond = mm_tail(mine, fkv_ref[:, 0:PAIR])
                        highest = jnp.maximum(highest, jnp.max(beyond, -1, keepdims=True))
                        beyond = jnp.exp(beyond - highest)
                    scores = jnp.exp(scores - highest)
                    total = jnp.sum(scores, -1, keepdims=True)
                    mixed = mm(scores.astype(BF16), kv_ref[0:end, PAIR : 2 * PAIR])
                    if far:
                        total = total + jnp.sum(beyond, -1, keepdims=True)
                        mixed = mixed + mm(beyond.astype(BF16), fkv_ref[:, PAIR : 2 * PAIR])
                    sums.append(mixed / total)
                    logs.append(jnp.broadcast_to(highest + jnp.log(total), (tile, PAIR)))
                o_ref[t * tile : end] = jnp.where(lane_of(0), sums[0], sums[1])
                l_ref[t * tile : end] = jnp.where(lane_of(0), logs[0], logs[1])

        @pl.when(s_ref[1] == 0)
        def _():
            run(False)

        @pl.when(s_ref[1] != 0)
        def _():
            run(True)

    spec = pl.BlockSpec((rows, PAIR), lambda i, s: (0, i))
    both = pl.BlockSpec((rows, 2 * PAIR), lambda i, s: (0, i))
    return call(
        body,
        "attend",
        (shaped((rows, width), F32), shaped((rows, width), F32)),
        (pairs,),
        [spec, both, both],
        (spec, spec),
    )(scalars, queries, near, far_side)


def attend_back(queries, near, far_side, grads, attended, logs, scalars, first, pairs):
    rows = queries.shape[0]
    tile = min(TILE, rows)
    width = pairs * PAIR

    def body(
        s_ref, q_ref, kv_ref, fkv_ref, d_ref, o_ref, l_ref,
        dq_ref, dkv_ref, fdkv_ref,
    ):
        offset = s_ref[1] * rows
        length = s_ref[2]

        def run(far):
            query = q_ref[...] * jnp.asarray(0.125, BF16)
            grad = d_ref[...]
            log_rows = jnp.transpose(l_ref[...])
            picker = jnp.where(
                lax.broadcasted_iota(jnp.int32, (8, PAIR), 1) // HEAD_DIM
                == lax.broadcasted_iota(jnp.int32, (8, PAIR), 0),
                1.0,
                0.0,
            ).astype(F32)
            dots = lax.dot_general(
                picker,
                grad.astype(F32) * o_ref[...],
                (((1,), (1,)), ((), ())),
                precision=lax.Precision.HIGHEST,
                preferred_element_type=F32,
            )
            blocks = [
                (kv_ref, dkv_ref, t * tile, t * tile, True)
                for t in range(rows // tile)
            ]
            if far:
                blocks += [
                    (fkv_ref, fdkv_ref, t * tile, 0, False)
                    for t in range(rows // tile)
                ]
            turned = [[jnp.zeros((HEAD_DIM, tile), F32) for _ in range(rows // tile)] for _ in range(2)]
            for pair_ref, dpair_ref, at, low, masked in blocks:
                key = pair_ref[at : at + tile, 0:PAIR]
                value = pair_ref[at : at + tile, PAIR : 2 * PAIR]
                key_turned = jnp.transpose(key)
                count = rows - low
                kgrads, vgrads = [], []
                if masked:
                    key_at = lax.broadcasted_iota(jnp.int32, (tile, count), 0) + at
                    place = lax.broadcasted_iota(jnp.int32, (tile, count), 1) + low
                    allowed = (key_at <= place) & (key_at + offset < length)
                for head in range(2):
                    lanes = lane_of(head)
                    mine = jnp.where(lanes, query[low:rows], jnp.zeros((), BF16))
                    mine_grad = jnp.where(lanes, grad[low:rows], jnp.zeros((), BF16))
                    scores = mm_tail(key, mine)
                    if masked:
                        scores = jnp.where(allowed, scores, MASKED)
                    base = head * HEAD_DIM
                    probs = jnp.exp(scores - log_rows[base : base + 1, low:rows])
                    prob_grad = mm_tail(value, mine_grad)
                    score_grad = (probs * (prob_grad - dots[head : head + 1, low:rows])).astype(BF16)
                    vgrads.append(mm(probs.astype(BF16), grad[low:rows]))
                    kgrads.append(mm(score_grad, query[low:rows]))
                    part = mm(key_turned[base : base + HEAD_DIM], score_grad)
                    for t in range(low // tile, rows // tile):
                        turned[head][t] = turned[head][t] + part[:, t * tile - low : (t + 1) * tile - low]
                dpair_ref[at : at + tile, 0:PAIR] = jnp.where(lane_of(0), kgrads[0], kgrads[1]).astype(dpair_ref.dtype)
                dpair_ref[at : at + tile, PAIR : 2 * PAIR] = jnp.where(lane_of(0), vgrads[0], vgrads[1]).astype(dpair_ref.dtype)
            for t in range(rows // tile):
                both = jnp.concatenate([turned[0][t], turned[1][t]], 0)
                dq_ref[t * tile : (t + 1) * tile] = (jnp.transpose(both) * 0.125).astype(BF16)

        @pl.when(s_ref[1] == 0)
        def _():
            run(False)
            fdkv_ref[...] = jnp.zeros_like(fdkv_ref)

        @pl.when(s_ref[1] != 0)
        def _():
            run(True)

    spec = pl.BlockSpec((rows, PAIR), lambda i, s: (0, i + first))
    both = pl.BlockSpec((rows, 2 * PAIR), lambda i, s: (0, i + first))
    own = pl.BlockSpec((rows, PAIR), lambda i, s: (0, i))
    own_both = pl.BlockSpec((rows, 2 * PAIR), lambda i, s: (0, i))
    return call(
        body,
        "attend_back",
        (shaped((rows, width), BF16), shaped((rows, 2 * width), F32), shaped((rows, 2 * width), BF16)),
        (pairs,),
        [spec, both, both, spec, spec, spec],
        (own, own_both, own_both),
    )(scalars, queries, near, far_side, grads, attended, logs)


def join(attended, inputs, parts, places, gains, scalars):
    rows, width = attended.shape
    tile = min(TILE, rows)
    flat = parts

    def body(s_ref, a_ref, x_ref, g_ref, *refs):
        pieces, (sub_ref, mid_ref, ffn_ref, w_ref) = refs[: len(flat)], refs[len(flat) :]

        @pl.when(pl.program_id(0) == 0)
        def _():
            if len(parts) == 2:
                put_rows(s_ref, pieces[0], pieces[1], places, w_ref, 0, width // pieces[0].shape[2])
            else:
                put_blocks(s_ref, pieces, places, w_ref, 0, width)

        hat, _ = norm_stats(a_ref[...])
        low = (hat * g_ref[1:2, :]).astype(BF16)
        sub_ref[...] = low
        middle = x_ref[...].astype(F32) + mm(low, w_ref[...])
        mid_ref[...] = middle
        hat, _ = norm_stats(middle)
        ffn_ref[...] = (hat * g_ref[2:3, :]).astype(BF16)

    spec = rows_of((tile, width))
    return call(
        body,
        "join",
        (
            shaped((rows, width), BF16),
            shaped((rows, width), F32),
            shaped((rows, width), BF16),
            shaped((width, width), BF16),
        ),
        (rows // tile,),
        [spec, spec, whole((8, width))] + [whole(p.shape) for p in flat],
        (spec,) * 3 + (whole((width, width)),),
    )(scalars, attended, inputs, gains, *flat)


def join_back(branch, far_branch, fgrad, far_fgrad, middle, cotangent, attended, weights, gains, scalars):
    rows, width = middle.shape
    tile = min(TILE, rows)
    steps = rows // tile

    def body(
        s_ref, b_ref, fb_ref, f_ref, ff_ref, m_ref, c_ref, a_ref, w_ref, g_ref,
        out_ref, mg_ref, ml_ref, ag_ref,
    ):
        step = pl.program_id(0)
        places = lax.broadcasted_iota(jnp.int32, (tile, 1), 0) + (step * tile + s_ref[1] * rows)
        kept = (places < s_ref[2]).astype(F32)
        middle = m_ref[...]
        branch = b_ref[...].astype(F32) + fb_ref[...].astype(F32)
        out_ref[...] = (kept * (middle + branch)).astype(BF16)
        hat, inverse = norm_stats(middle)
        grad = f_ref[...].astype(F32) + ff_ref[...].astype(F32)
        middle_grad = c_ref[...].astype(F32) * kept + norm_back(grad, g_ref[2:3, :], hat, inverse)
        mg_ref[...] = middle_grad
        low = middle_grad.astype(BF16)
        ml_ref[...] = low
        sub_grad = mm_tail(low, w_ref[...])
        hat, inverse = norm_stats(a_ref[...])
        ag_ref[...] = norm_back(sub_grad, g_ref[1:2, :], hat, inverse).astype(BF16)

    spec = rows_of((tile, width))
    return call(
        body,
        "join_back",
        (
            shaped((rows, width), BF16),
            shaped((rows, width), F32),
            shaped((rows, width), BF16),
            shaped((rows, width), BF16),
        ),
        (steps,),
        [spec] * 7 + [whole((width, width)), whole((8, width))],
        (spec,) * 4,
    )(scalars, branch, far_branch, fgrad, far_fgrad, middle, cotangent, attended, weights, gains)


def two_sided(tile, width, steps):
    near = pl.BlockSpec((tile, width), lambda i, s: (jnp.minimum(i, steps - 1), 0))
    far = pl.BlockSpec((tile, width), lambda i, s: (jnp.maximum(i - steps, 0), 0))
    return near, far


def stat_rows(first, second):
    lanes = lax.broadcasted_iota(jnp.int32, (first.shape[0], 128), 1)
    return jnp.transpose(jnp.where(lanes == 0, first, jnp.where(lanes == 1, second, 0.0)))[0:8]


def stat_columns(mine, other):
    both = jnp.transpose(mine + other)
    return both[:, 0:1], both[:, 1:2]


def unit_norm(mine, other, total):
    sums, squares = stat_columns(mine, other)
    center = sums / total
    return center, lax.rsqrt(squares / total - center * center + EPSILON)


def fold(value):
    out = value[:, 0:128]
    for at in range(128, value.shape[1], 128):
        out = out + value[:, at : at + 128]
    return out


def to_side(near, near_ref, far_ref, value):
    low = value.astype(BF16)

    @pl.when(near)
    def _():
        near_ref[...] = low

    @pl.when(jnp.logical_not(near))
    def _():
        far_ref[...] = low


def stats_of(tile):
    return pl.BlockSpec((8, tile), lambda i, s: (0, i))


def other_stats(tile, steps):
    return pl.BlockSpec((8, tile), lambda i, s: (0, lax.rem(i + steps, 2 * steps)))


def ffn_in(near, far, parts, places, units, scalars):
    rows, width = near.shape
    pieces = [piece for part in parts for piece in part]
    cuts = [part[0].shape[2] for part in parts]
    cuts[-1] = units - sum(cuts[:-1])
    tile = min(TILE, rows)
    steps = rows // tile
    chunk = 256

    def body(s_ref, n_ref, f_ref, *refs):
        blocks, (act_ref, slope_ref, stat_ref, w_ref) = refs[: len(pieces)], refs[len(pieces) :]

        @pl.when(pl.program_id(0) == 0)
        def _():
            at = 0
            for k, part in enumerate(parts):
                put_blocks(s_ref, blocks[at : at + len(part)], places[k], w_ref, sum(cuts[:k]), cuts[k])
                at += len(part)

        low = jnp.where(pl.program_id(0) < steps, n_ref[...], f_ref[...])
        sums = jnp.zeros((tile, 128), F32)
        squares = jnp.zeros((tile, 128), F32)
        for at in range(0, units, chunk):
            pre = mm(low, w_ref[:, at : at + chunk])
            cdf = 0.5 * (1.0 + lax.erf(pre * 0.7071067811865476))
            pdf = 0.3989422804014327 * jnp.exp(-0.5 * pre * pre)
            act = pre * cdf
            act_ref[:, at : at + chunk] = act
            slope_ref[:, at : at + chunk] = (cdf + pre * pdf).astype(slope_ref.dtype)
            sums = sums + fold(act)
            squares = squares + fold(act * act)
        stat_ref[...] = stat_rows(
            jnp.sum(sums, -1, keepdims=True), jnp.sum(squares, -1, keepdims=True)
        )

    near_spec, far_spec = two_sided(tile, width, steps)
    return call(
        body,
        "ffn_in",
        (
            shaped((2 * rows, units), F32),
            shaped((2 * rows, units), BF16),
            shaped((8, 2 * rows), F32),
            shaped((width, units), BF16),
        ),
        (2 * steps,),
        [near_spec, far_spec] + [whole(p.shape) for p in pieces],
        (rows_of((tile, units)), rows_of((tile, units)), stats_of(tile), whole((width, units))),
    )(scalars, near, far, *pieces)


def ffn_out(act, stats, far_stats, gain, near_grad, far_grad, weights, scalars, order):
    rows, width = near_grad.shape
    units = act.shape[1]
    tile = min(TILE, rows)
    steps = rows // tile
    depth = width // len(order)
    chunk = 256

    def body(s_ref, a_ref, st_ref, fs_ref, g_ref, n_ref, f_ref, w_ref, b_ref, fb_ref, stat_ref, out_ref, stash, tilt):
        step = pl.program_id(0)
        weight = w_ref.at[0]

        @pl.when(step == 0)
        def _():
            tilt[...] = mm_tail(jnp.broadcast_to(g_ref[...], (8, units)).astype(BF16), weight[...])

        center, inverse = unit_norm(st_ref[...], fs_ref[...], 2 * units)
        at_row = pl.multiple_of(step * tile, tile)
        for at in range(0, units, chunk):
            hat = (a_ref[:, at : at + chunk] - center) * inverse
            stash[pl.ds(at_row, tile), at : at + chunk] = (hat * g_ref[:, at : at + chunk]).astype(BF16)
        branch = mm_tail(stash[pl.ds(at_row, tile), :], weight[...])
        to_side(step < steps, b_ref, fb_ref, branch)
        inside = pl.multiple_of(lax.rem(step, steps) * tile, tile)
        grad = jnp.where(step < steps, n_ref[pl.ds(inside, tile)], f_ref[pl.ds(inside, tile)]).astype(F32)
        stat_ref[...] = stat_rows(
            jnp.sum(fold(grad * tilt[0:1, :]), -1, keepdims=True),
            jnp.sum(fold(grad * branch), -1, keepdims=True),
        )

        @pl.when(step == 2 * steps - 1)
        def _():
            near_turned, far_turned = jnp.transpose(n_ref[...]), jnp.transpose(f_ref[...])
            for at in range(0, units, 512):
                part = mm(near_turned, stash[0:rows, at : at + 512]) + mm(far_turned, stash[rows:, at : at + 512])
                for to, block in enumerate(order):
                    out_ref[to * depth : (to + 1) * depth, at : at + 512] = part[
                        block * depth : (block + 1) * depth
                    ].astype(BF16)

    return call(
        body,
        "ffn_out",
        (
            shaped((rows, width), BF16),
            shaped((rows, width), BF16),
            shaped((8, 2 * rows), F32),
            shaped((width, units), BF16),
        ),
        (2 * steps,),
        [
            rows_of((tile, units)),
            stats_of(tile),
            other_stats(tile, steps),
            whole((1, units)),
            whole((rows, width)),
            whole((rows, width)),
            whole((1, width, units)),
        ],
        two_sided(tile, width, steps) + (stats_of(tile), whole((width, units))),
        scratch=[pltpu.VMEM((2 * rows, units), BF16), pltpu.VMEM((8, width), F32)],
    )(scalars, act, stats, far_stats, gain, near_grad, far_grad, weights)


def ffn_back(
    act, slope, stats, far_stats, grads, far_grads, gain, near_grad, far_grad, near, far, out_weights, in_weights, scalars, blocks
):
    rows, width = near.shape
    units = act.shape[1]
    tile = min(TILE, rows)
    steps = rows // tile
    depth = width // blocks
    chunk = 256
    piece = units // 4

    def body(
        s_ref, a_ref, sl_ref, st_ref, fs_ref, gt_ref, fg_ref, g_ref, ng_ref, fgr_ref, n_ref, f_ref, wo_ref, wi_ref,
        b_ref, fb_ref, four_ref, *rest,
    ):
        outs, (stash, fourth, total) = rest[:-3], rest[-3:]
        step = pl.program_id(0)
        center, inverse = unit_norm(st_ref[...], fs_ref[...], 2 * units)
        first, second = stat_columns(gt_ref[...], fg_ref[...])
        first, second = first / (2 * units), second / (2 * units)
        at_row = pl.multiple_of(step * tile, tile)
        inside = pl.multiple_of(lax.rem(step, steps) * tile, tile)
        grad = jnp.where(step < steps, ng_ref[pl.ds(inside, tile)], fgr_ref[pl.ds(inside, tile)])

        @pl.when(step == 0)
        def _():
            fourth[...] = jnp.zeros_like(fourth)

        for at in range(0, units, chunk):
            normed = mm(grad, wo_ref[0, :, at : at + chunk])
            hat = (a_ref[:, at : at + chunk] - center) * inverse
            fourth[:, at : at + chunk] += jnp.sum((normed * hat).reshape(tile // 8, 8, chunk), 0)
            act_grad = inverse * (normed * g_ref[:, at : at + chunk] - first - hat * second)
            stash[pl.ds(at_row, tile), at : at + chunk] = (
                act_grad * sl_ref[:, at : at + chunk].astype(F32)
            ).astype(BF16)
        to_side(step < steps, b_ref, fb_ref, mm_tail(stash[pl.ds(at_row, tile), :], wi_ref[...]))

        @pl.when(step == 2 * steps - 1)
        def _():
            value = jnp.sum(fourth[...], 0, keepdims=True)
            four_ref[...] = jnp.broadcast_to(value, four_ref.shape)
            near_turned, far_turned = jnp.transpose(n_ref[...]), jnp.transpose(f_ref[...])
            for at in range(0, units, piece):
                part = mm(near_turned, stash[0:rows, at : at + piece]) + mm(far_turned, stash[rows:, at : at + piece])
                if blocks == 1:
                    outs[0][:, at : at + piece] = part.astype(BF16)
                else:
                    total[...] = part
                    order = 0 if at < units // 2 else 1
                    inside = at - order * (units // 2)
                    for block in range(blocks):
                        slot = slot_of(block ^ s_ref[0], order, blocks)
                        low = total[block * depth : (block + 1) * depth].astype(BF16)

                        @pl.when(slot < blocks // 2)
                        def _():
                            outs[0][pl.ds(pl.multiple_of(slot * depth, 16), depth), at : at + piece] = low

                        @pl.when(slot >= blocks // 2)
                        def _():
                            row = pl.multiple_of((slot - blocks // 2) * depth, 16)
                            outs[1 + order][pl.ds(row, depth), inside : inside + piece] = low
            if blocks > 1:
                high = value.astype(BF16)
                rest_of = (value - high.astype(F32)).astype(BF16)
                at_line = lax.broadcasted_iota(jnp.int32, (EXTRA, units), 0)
                extra = jnp.where(at_line == 0, high.astype(F32), jnp.where(at_line == 1, rest_of.astype(F32), 0.0))
                extra = extra.astype(BF16)
                outs[1][width // 2 : width // 2 + EXTRA] = extra[:, : units // 2]
                outs[2][width // 2 : width // 2 + EXTRA] = extra[:, units // 2 :]

    wide = rows_of((tile, units))
    crossing = (width // 2 + EXTRA, units // 2)
    shapes = ((width, units),) if blocks == 1 else ((width // 2, units), crossing, crossing)
    return call(
        body,
        "ffn_back",
        (shaped((rows, width), BF16), shaped((rows, width), BF16), shaped((8, units), F32))
        + tuple(shaped(shape, BF16) for shape in shapes),
        (2 * steps,),
        [
            wide, wide, stats_of(tile), other_stats(tile, steps), stats_of(tile), other_stats(tile, steps),
            whole((1, units)),
        ]
        + [whole((rows, width))] * 4
        + [whole((1, width, units)), whole((width, units))],
        two_sided(tile, width, steps) + (whole((8, units)),) + tuple(whole(shape) for shape in shapes),
        scratch=[
            pltpu.VMEM((2 * rows, units), BF16),
            pltpu.VMEM((8, units), F32),
            pltpu.VMEM((width, piece), F32),
        ],
    )(
        scalars, act, slope, stats, far_stats, grads, far_grads, gain, near_grad, far_grad, near, far, out_weights,
        in_weights,
    )


def slot_of(position, order, blocks):
    if blocks < 4:
        return position
    low = (position >> order) & 1
    high = (position >> (1 - order)) & 1
    return low * (blocks // 2) + high * (blocks // 4) + (position >> 2)


def project_grads(normed, dq, dkv, far_dkv, extra, parts, scalars, blocks):
    rows, width = normed.shape
    cols = dq.shape[1]
    depth = width // blocks
    own = depth // 2
    total = 3 * cols + (width if extra else 0)
    pairs = cols // PAIR
    shape = (blocks, own, total) if blocks > 1 else (1, width, total)

    def body(s_ref, n_ref, q_ref, kv_ref, fkv_ref, *refs):
        if extra:
            left_ref, right_ref = refs[:2]
            refs = refs[2:]
        low_ref, *outs, grad_ref = refs
        me, core = s_ref[0], s_ref[1]
        near = core == 0
        both = kv_ref[...] + jnp.where(near, fkv_ref[...].astype(F32), 0.0)
        low_ref[:, 0:cols] = q_ref[...]
        for pair in range(pairs):
            for which in range(2):
                to = (1 + which) * cols + pair * PAIR
                at = (2 * pair + which) * PAIR
                low_ref[:, to : to + PAIR] = both[:, at : at + PAIR].astype(BF16)
        turned = jnp.transpose(n_ref[...])
        grad_ref[:, 0 : 3 * cols] = mm(turned, low_ref[...])
        if extra:
            grad_ref[:, 3 * cols : total] = mm_lead(left_ref[...], right_ref[...])
        if blocks == 1:
            outs[0][0] = grad_ref[...].astype(BF16)
            return
        for side, out in ((0, outs[0]), (1, outs[1])):
            owner = core if side == 0 else 1 - core
            for block in range(blocks):
                position = block ^ me
                row = pl.multiple_of(block * depth + owner * own, 8)
                for order, start, end in parts:
                    slot = slot_of(position, order, blocks)
                    out[slot, :, start:end] = grad_ref[pl.ds(row, own), start:end].astype(BF16)

    more = list(extra) if extra else []
    pieces = 1 if blocks == 1 else 2
    return call(
        body,
        "project_grads",
        (shaped((rows, 3 * cols), BF16),) + (shaped(shape, BF16),) * pieces,
        (1,),
        [whole((rows, width)), whole((rows, cols)), whole((rows, 2 * cols)), whole((rows, 2 * cols))]
        + [whole((rows, width))] * len(more),
        (whole((rows, 3 * cols)),) + (whole(shape),) * pieces,
        scratch=[pltpu.VMEM((width, total), F32)],
    )(scalars, normed, dq, dkv, far_dkv, *more)


def project_back(lows, inputs, middle_grad, weights, gains, scalars):
    rows, width = inputs.shape
    tile = min(TILE, rows)
    sizes = [low.shape[1] // 3 for low in lows]

    def body(s_ref, *refs):
        low_refs, (x_ref, m_ref, w_ref, g_ref, out_ref) = refs[: len(lows)], refs[len(lows) :]
        hat, inverse = norm_stats(x_ref[...].astype(F32))
        grad = jnp.zeros((tile, width), F32)
        at = 0
        for low_ref, size in zip(low_refs, sizes):
            for which in range(3):
                base = which * width + at
                grad = grad + mm_tail(
                    low_ref[:, which * size : (which + 1) * size], w_ref[:, base : base + size]
                )
            at += size
        out_ref[...] = (m_ref[...] + norm_back(grad, g_ref[0:1, :], hat, inverse)).astype(BF16)

    spec = rows_of((tile, width))
    return call(
        body,
        "project_back",
        shaped((rows, width), BF16),
        (rows // tile,),
        [rows_of((tile, 3 * size)) for size in sizes]
        + [spec, spec, whole((width, 3 * width)), whole((8, width))],
        spec,
    )(scalars, *lows, inputs, middle_grad, weights, gains)


CHIPS = ("outer", "inner")
CORES = "tensor"


def other_core(array):
    return lax.ppermute(array, CORES, [(0, 1), (1, 0)])


def exchange(array, mask, chips):
    return lax.ppermute(array, CHIPS, [(i, i ^ mask) for i in range(chips)])


def bit_count(chips):
    return chips.bit_length() - 1


def by_core(mine, other, axis):
    core = lax.axis_index(CORES)
    return jnp.where(
        core == 0,
        jnp.concatenate([mine, other], axis),
        jnp.concatenate([other, mine], axis),
    )


def after(value, *others):
    return lax.optimization_barrier((value,) + others)[0]


def gather_outer(shard, chips):
    places = list(range(0, chips, 4))
    return jnp.stack([shard] + [exchange(shard, mask, chips) for mask in places[1:]], 0), places


def widen(pieces, places, mask, chips):
    held = pieces[0] if len(pieces) == 1 else jnp.concatenate(pieces, 0)
    return pieces + [exchange(held, mask, chips)], places + [p | mask for p in places]


def on_device(
    inputs,
    cotangent,
    lengths,
    query_key,
    value_proj,
    output_proj,
    hidden_in,
    hidden_out,
    first_gain,
    second_gain,
    third_gain,
    fourth_gain,
):
    rows, width = inputs.shape[1:]
    chips = lax.axis_size(CHIPS)
    inner = lax.axis_size("inner")
    chip = lax.axis_index(CHIPS)
    core = lax.axis_index(CORES)
    barrier = lax.optimization_barrier
    depth = width // chips
    pairwise = chips & (chips - 1) == 0 and chips >= 4 and depth % 16 == 0
    series = inputs[0]
    scalars = jnp.stack([chip if pairwise else jnp.zeros_like(chip), core, lengths[0]]).astype(jnp.int32)
    scalars = jnp.concatenate([scalars, jnp.zeros((5,), jnp.int32)])

    gain_columns = jnp.stack([first_gain, second_gain, third_gain], 1)
    gain_columns = jnp.pad(gain_columns, ((0, 0), (0, 256 - 3)))
    shard = jnp.concatenate([query_key, value_proj, gain_columns], 1)
    half = shard.shape[1]
    units = hidden_in.shape[1]
    if pairwise:
        stack, places = gather_outer(shard, chips)
        cut = -(-half // 256) * 128
        o_folded = jnp.concatenate([output_proj[:, : width // 2], output_proj[:, width // 2 :]], 0)
        late_shard = jnp.concatenate([hidden_in, o_folded], 1)
        late_out = hidden_out.T
        stack, late_shard = barrier((stack, late_shard))
        out_weights_ff = lax.all_gather(late_out, CHIPS, axis=0, tiled=True)[None]
        first, first_places = widen([stack[:, :, :cut]], places, 2, chips)
        second, second_places = widen([stack[:, :, cut:]], places, 1, chips)
        late, late_places = gather_outer(late_shard, chips)
        first[-1], second[-1] = barrier((first[-1], second[-1]))
        first, first_places = widen(first, first_places, 1, chips)
        second, second_places = widen(second, second_places, 2, chips)
        first[-1], second[-1], late = barrier((first[-1], second[-1], late))
        late_cut = -(-late.shape[2] // 256) * 128
        in_first, in_first_places = widen([late[:, :, :late_cut]], late_places, 1, chips)
        in_second, in_second_places = widen([late[:, :, late_cut:]], late_places, 2, chips)
        mine = [jnp.concatenate(first, 0), jnp.concatenate(second, 0)]
        parts = [[p, other_core(p)] for p in mine]
        part_places = [first_places, second_places]
    else:
        gathered = lax.all_gather(shard, CHIPS + (CORES,), axis=0, tiled=True)
        parts, part_places = [[gathered[None]]], [[0]]
        in_parts = [[lax.all_gather(hidden_in, CHIPS, axis=0, tiled=True)[None]]]
        in_part_places = [[0]]
        out_weights = lax.all_gather(output_proj, CHIPS + (CORES,), axis=0, tiled=True)
        out_weights_ff = lax.all_gather(hidden_out.T, CHIPS, axis=0, tiled=True)[None]

    kept = (core * rows + jnp.arange(rows) < lengths[0])[:, None]
    near_grad = jnp.where(kept, cotangent[0], jnp.zeros((), BF16))
    far_grad = other_core(near_grad)

    if pairwise:
        series, in_first[0], in_second[0] = barrier((series, in_first[0], in_second[0]))
    queries, near_kv, normed, weights, gains = project(series, parts, part_places, scalars)
    if pairwise:
        near_kv, in_first[-1], in_second[-1] = barrier((near_kv, in_first[-1], in_second[-1]))
    far_kv = lax.ppermute(near_kv, CORES, [(0, 1)])
    if pairwise:
        in_first, in_first_places = widen(in_first, in_first_places, 2, chips)
        in_second, in_second_places = widen(in_second, in_second_places, 1, chips)
    attended, logs = attend(queries, near_kv, far_kv, scalars)
    if pairwise:
        attended, in_first[-1], in_second[-1] = barrier((attended, in_first[-1], in_second[-1]))
        in_parts = [in_first, in_second]
        in_part_places = [in_first_places, in_second_places]
        extra_columns = units - late_cut
        o_mine = jnp.concatenate(in_second, 0)[:, :, extra_columns:]
        out_parts = [o_mine, other_core(o_mine)]
        sub_low, middle, near, out_weights = join(attended, series, out_parts, in_second_places, gains, scalars)
    else:
        sub_low, middle, near, out_weights = join(attended, series, [out_weights[None]], [0], gains, scalars)
    far = other_core(near)

    if pairwise:
        far, out_weights_ff = barrier((far, out_weights_ff))
    act, slope, stats, in_weights = ffn_in(near, far, in_parts, in_part_places, units, scalars)
    far_stats = other_core(stats)
    outer = chips // inner
    order = list(range(chips))
    if pairwise:
        order = [o * inner + i for i in range(inner) for o in range(outer)]
    gain_four = fourth_gain.astype(F32)[None, :]
    branch, branch_sent, grad_stats, out_payload = ffn_out(
        act, stats, far_stats, gain_four, near_grad, far_grad, out_weights_ff, scalars, order
    )
    if pairwise:
        out_payload = lax.psum_scatter(out_payload, "inner", scatter_dimension=0, tiled=True)
    else:
        out_payload = lax.psum_scatter(out_payload, CHIPS, scatter_dimension=0, tiled=True)
    far_grad_stats = other_core(grad_stats)
    far_branch = other_core(branch_sent)
    blocks = chips if pairwise else 1
    ffn_grad, ffn_grad_sent, fourth_term, *in_payload = ffn_back(
        act, slope, stats, far_stats, grad_stats, far_grad_stats, gain_four, near_grad, far_grad, near, far,
        out_weights_ff, in_weights, scalars, blocks,
    )
    far_ffn_grad = other_core(ffn_grad_sent)
    if pairwise:
        got = [exchange(in_payload[1], 1, chips), exchange(in_payload[2], 2, chips)]
    outputs, middle_grad, middle_low, attended_low = join_back(
        branch, far_branch, ffn_grad, far_ffn_grad, middle, near_grad, attended, out_weights, gains, scalars
    )

    pairs = width // PAIR
    extra = (sub_low, middle_low)
    if pairwise:
        columns = 4 * width
        cut = columns // 2
        middle, lower = chips // 2, chips // 4
        count = width // 2
        dq, dkv, far_dkv = attend_back(queries, near_kv, far_kv, attended_low, attended, logs, scalars, 0, pairs)
        got[0], got[1], out_payload, far_dkv = barrier((got[0], got[1], out_payload, far_dkv))
        far_dkv = lax.ppermute(far_dkv, CORES, [(1, 0)])
        out_payload = lax.psum_scatter(out_payload, "outer", scatter_dimension=0, tiled=True)
        in_kept, fourth = add_parts(in_payload[0][: count // 2], fourth_term[0:1], got, 0, count)
        in_sent, _ = add_parts(in_payload[0][count // 2 :], fourth_term[0:1], got, count // 2, count)
        rows_low = low_rows(fourth)
        sent = [
            jnp.concatenate([in_sent[:, : units // 2], rows_low[:, : units // 2]], 0),
            jnp.concatenate([in_sent[:, units // 2 :], rows_low[:, units // 2 :]], 0),
        ]
        far_dkv, sent[0], sent[1], in_kept = barrier((far_dkv, sent[0], sent[1], in_kept))
        got = [exchange(sent[0], 2, chips), exchange(sent[1], 1, chips)]
        low, keep, send = project_grads(
            normed, dq, dkv, far_dkv, extra, ((0, 0, cut), (1, cut, columns)), scalars, chips
        )
        middle_grad, keep, send = barrier((middle_grad, keep, send))
        other = other_core(send)
        inputs_grad = project_back([low], series, middle_grad, weights, gains, scalars)
        inputs_grad, other, got[0], got[1] = barrier((inputs_grad, other, got[0], got[1]))
        upper_one = add_low(keep[middle:, :, :cut], other[middle:, :, :cut])
        upper_two = add_low(keep[middle:, :, cut:], other[middle:, :, cut:])
        upper_one, upper_two = barrier((upper_one, upper_two))
        got_one, got_two = exchange(upper_one, 1, chips), exchange(upper_two, 2, chips)
        in_held, fourth = add_parts(in_kept, fourth, got, 0, count // 2)
        in_held = in_held.reshape(chips // 4, depth, units)
        sends = barrier(tuple(outer_sends(in_held, fourth)))
        got_one, got_two, *sends = barrier((got_one, got_two, *sends))
        in_got = exchange_outer(sends, chips)
        sent_first = sum_low(keep[lower:middle, :, :cut], other[lower:middle, :, :cut], got_one[lower:])
        sent_second = sum_low(keep[lower:middle, :, cut:], other[lower:middle, :, cut:], got_two[lower:])
        sent_first, sent_second = barrier((sent_first, sent_second))
        got_first, got_second = exchange(sent_first, 2, chips), exchange(sent_second, 1, chips)
        kept = sum_low(keep[:lower], other[:lower], jnp.concatenate([got_one[:lower], got_two[:lower]], -1))
        got_first, got_second, kept, out_payload = barrier((got_first, got_second, kept, out_payload))
        both = add_low(kept, jnp.concatenate([got_first, got_second], -1))
        both_sends = barrier(tuple(outer_sends(both, None)))
        both_got = exchange_outer(both_sends, chips)
        both_got[0], *in_got = barrier((both_got[0], *in_got))
        in_payload = in_held[0].astype(F32)
        for piece in in_got:
            in_payload = in_payload + piece[:depth].astype(F32)
            fourth = add_rows(fourth, piece[depth:])
        third_part = jnp.sum(hidden_in.astype(F32) * in_payload, 1, keepdims=True)
        third_part = jnp.broadcast_to(third_part, (depth, 128))
        third_part = third_part + other_core(third_part)
        *both_got, third_part = barrier((*both_got, third_part))
        total = both[0].astype(F32)
        for piece in both_got:
            total = total + piece.astype(F32)
        large = total
    else:
        dq, dkv, far_dkv = attend_back(queries, near_kv, far_kv, attended_low, attended, logs, scalars, 0, pairs)
        far_dkv = lax.ppermute(far_dkv, CORES, [(1, 0)])
        low, mine = project_grads(normed, dq, dkv, far_dkv, extra, None, scalars, 1)
        mine = lax.psum_scatter(mine[0], CHIPS, scatter_dimension=0, tiled=True).astype(F32)
        mine = lax.psum(mine, CORES)
        inputs_grad = project_back([low], series, middle_grad, weights, gains, scalars)
        in_payload = lax.psum_scatter(in_payload[0], CHIPS, scatter_dimension=0, tiled=True).astype(F32)
        fourth = lax.psum(fourth_term[0:1], CHIPS)
        large = lax.dynamic_slice_in_dim(mine, core * (depth // 2), depth // 2, 0)
        third_part = lax.psum(jnp.sum(hidden_in.astype(F32) * in_payload, 1, keepdims=True), CORES)
    hidden_out_sum = out_payload.astype(F32).T
    hidden_in_sum = in_payload
    third_sum = lax.dynamic_slice_in_dim(third_part[:, 0], core * (depth // 2), depth // 2) / third_gain.astype(F32)
    qk_sum, value_sum, output_sum = large[:, : 2 * width], large[:, 2 * width : 3 * width], large[:, 3 * width :]
    first_sum = (
        jnp.sum(query_key.astype(F32) * qk_sum, 1) + jnp.sum(value_proj.astype(F32) * value_sum, 1)
    ) / first_gain.astype(F32)
    second_sum = jnp.sum(output_proj.astype(F32) * output_sum, 1) / second_gain.astype(F32)
    return (
        outputs[None],
        inputs_grad[None],
        qk_sum,
        value_sum,
        output_sum,
        hidden_in_sum,
        hidden_out_sum,
        first_sum,
        second_sum,
        third_sum,
        fourth[0],
    )


def add_low(kept, got):
    return (kept.astype(F32) + got.astype(F32)).astype(BF16)


def add_rows(value, rows):
    return value + (rows[0:1].astype(F32) + rows[1:2].astype(F32))


def low_rows(vector):
    high = lax.reduce_precision(vector, 8, 7)
    rest = lax.reduce_precision(vector - high, 8, 7)
    return jnp.concatenate([high, rest, jnp.zeros((EXTRA - 2, vector.shape[1]), F32)], 0).astype(BF16)


def outer_sends(held, vector):
    rows = [] if vector is None else [low_rows(vector)]
    return [jnp.concatenate([held[at]] + rows, 0) if rows else held[at] for at in range(1, held.shape[0])]


def exchange_outer(sends, chips):
    return [exchange(send, 4 * (at + 1), chips) for at, send in enumerate(sends)]


def add_parts(kept, vector, got, start, count):
    part = jnp.concatenate([piece[start : start + kept.shape[0]] for piece in got], 1)
    rows = jnp.concatenate([piece[count:] for piece in got], 1)
    return add_low(kept, part), add_rows(vector, rows)


def sum_low(*arrays):
    total = arrays[0].astype(F32)
    for array in arrays[1:]:
        total = total + array.astype(F32)
    return total.astype(BF16)


def solution(mesh):
    chips, cores = mesh.devices.shape
    inner = 4 if chips % 4 == 0 else 1
    split = Mesh(mesh.devices.reshape(chips // inner, inner, cores), CHIPS + (CORES,))
    every = CHIPS + (CORES,)
    return jax.shard_map(
        on_device,
        mesh=split,
        in_specs=(
            P(CHIPS, CORES, None),
            P(CHIPS, CORES, None),
            P(CHIPS),
            P(every, None),
            P(every, None),
            P(every, None),
            P(CHIPS, CORES),
            P(CORES, CHIPS),
            P(every),
            P(every),
            P(every),
            P(CORES),
        ),
        out_specs=(
            P(CHIPS, CORES, None),
            P(CHIPS, CORES, None),
            P(every, None),
            P(every, None),
            P(every, None),
            P(CHIPS, CORES),
            P(CORES, CHIPS),
            P(every),
            P(every),
            P(every),
            P(CORES),
        ),
        check_vma=False,
    )
```

profile of v0, /device:TPU:0, one launch (start us, length us, event | category | flops | bytes accessed | tf_op | source)
XLA Modules:
  0.0 274.6 jit_solution(18298739525186595901)
XLA Ops:
  9.0 4.1 %collective-permute-start.1 = (bf16[24,2560]{1,0:T(8,128)(2,1)S(1)}, bf16[24,2560]{1,0:T(8,128)(2,1)S(1)}, u32[]{:S(2)}, u32[]{:S(2)}) collective-permute-start(bf16[24,2560]{1,0:T(8,128)(2,1)S(1)} %get-tuple-element.236), channel_id=1, source_target_pairs={{0,16},{2,18},{4,20},{6,22},{8,24},{10,26},{12,28},{14,30},{16,0},... | collective-permute-start | bytes 368648 | tf_op jit(solution)/shard_map/ppermute | solution.py:771
  16.3 4.4 %collective-permute-done.1 = bf16[24,2560]{1,0:T(8,128)(2,1)S(1)} collective-permute-done((bf16[24,2560]{1,0:T(8,128)(2,1)S(1)}, bf16[24,2560]{1,0:T(8,128)(2,1)S(1)}, u32[]{:S(2)}, u32[]{:S(2)}) %collective-permute-start.1) | collective-permute-done | bytes 122912 | tf_op jit(solution)/shard_map/ppermute | solution.py:771
  26.0 3.8 %collective-permute-done.4 = bf16[4,24,1280]{2,1,0:T(8,128)(2,1)S(1)} collective-permute-done((bf16[4,24,1280]{2,1,0:T(8,128)(2,1)S(1)}, bf16[4,24,1280]{2,1,0:T(8,128)(2,1)S(1)}, u32[]{:S(2)}, u32[]{:S(2)}) %collective-permute-start.4) | collective-permute-done | bytes 245792 | tf_op jit(solution)/shard_map/ppermute | solution.py:771
  33.2 2.4 collective-permute-start.9
  35.6 2.8 %collective-permute-start.8 = (bf16[48,1920]{1,0:T(8,128)(2,1)S(1)}, bf16[48,1920]{1,0:T(8,128)(2,1)S(1)}, u32[]{:S(2)}, u32[]{:S(2)}) collective-permute-start(bf16[48,1920]{1,0:T(8,128)(2,1)S(1)} %maximum_maximum_fusion), channel_id=1, source_target_pairs={{0,16},{2,18},{4,20},{6,22},{8,24},{10,26},{12,28},{14,30},{16,0},... | collective-permute-start | bytes 552968 | tf_op jit(solution)/shard_map/ppermute | solution.py:771
  41.3 10.5 %collective-permute-done.8 = bf16[48,1920]{1,0:T(8,128)(2,1)S(1)} collective-permute-done((bf16[48,1920]{1,0:T(8,128)(2,1)S(1)}, bf16[48,1920]{1,0:T(8,128)(2,1)S(1)}, u32[]{:S(2)}, u32[]{:S(2)}) %collective-permute-start.8) | collective-permute-done | bytes 184352 | tf_op jit(solution)/shard_map/ppermute | solution.py:771
  57.2 8.3 %project.1 = (bf16[512,768]{1,0:T(8,128)(2,1)}, bf16[512,1536]{1,0:T(8,128)(2,1)}, bf16[512,768]{1,0:T(8,128)(2,1)}, bf16[768,2304]{1,0:T(8,128)(2,1)}, f32[8,768]{1,0:T(8,128)}) custom-call(s32[8]{0:T(128)} %pad_add_fusion.s_ref, bf16[512,768]{1,0:T(8,128)(2,1)} %bitcast.40, bf16[16,24,1280]{2,1,0:T(8,128)(2,1)} %copy-done.3, ...), custom_call_target="tpu_custom_call" | custom-call | flops 1 | bytes 1476000 | tf_op jit(solution)/shard_map/project/pallas_call | solution.py:152
  65.5 2.3 collective-permute-start.14
  72.5 10.9 %attend.1 = (f32[512,768]{1,0:T(8,128)}, f32[512,768]{1,0:T(8,128)}) custom-call(s32[8]{0:T(128)} %pad_add_fusion.s_ref, bf16[512,768]{1,0:T(8,128)(2,1)} %get-tuple-element.114.q_ref, bf16[512,1536]{1,0:T(8,128)(2,1)} %get-tuple-element.116.kv_ref, bf16[512,1536]{1,0:T(8,128)(2,1)} %copy-done.1), custom_call_target="tpu_custom_call" | custom-call | flops 1 | bytes 2767500 | tf_op jit(solution)/shard_map/attend/pallas_call | solution.py:223
  83.5 7.5 %collective-permute-done.16.refs_5_ = bf16[8,48,896]{2,1,0:T(8,128)(2,1)S(1)} collective-permute-done((bf16[8,48,896]{2,1,0:T(8,128)(2,1)}, bf16[8,48,896]{2,1,0:T(8,128)(2,1)S(1)}, u32[]{:S(2)}, u32[]{:S(2)}) %collective-permute-start.16) | collective-permute-done | bytes 688160 | tf_op jit(solution)/shard_map/ppermute | solution.py:771
  95.4 5.2 %join.1 = (bf16[512,768]{1,0:T(8,128)(2,1)}, f32[512,768]{1,0:T(8,128)}, bf16[512,768]{1,0:T(8,128)(2,1)}, bf16[768,768]{1,0:T(8,128)(2,1)}) custom-call(s32[8]{0:T(128)} %pad_add_fusion.s_ref, f32[512,768]{1,0:T(8,128)} %get-tuple-element.122.a_ref.o_ref, bf16[512,768]{1,0:T(8,128)(2,1)} %bitcast.41, f32[8,768]{1,0:T(8,128)} %get-tuple-element.123.g_ref.refs_4_, ...), custom_call_target="tpu_custom_call" | custom-call | flops 1 | bytes 922500 | tf_op jit(solution)/shard_map/join/pallas_call | solution.py:351
  101.3 2.4 all-gather.2.cloned.1.call-done
  104.7 10.0 %ffn_in.1 = (f32[1024,1536]{1,0:T(8,128)}, bf16[1024,1536]{1,0:T(8,128)(2,1)}, f32[8,1024]{1,0:T(8,128)}, bf16[768,1536]{1,0:T(8,128)(2,1)}) custom-call(s32[8]{0:T(128)} %pad_add_fusion.s_ref, bf16[512,768]{1,0:T(8,128)(2,1)} %get-tuple-element.125.n_ref, bf16[512,768]{1,0:T(8,128)(2,1)} %copy-done.6, bf16[4,48,1024]{2,1,0:T(8,128)(2,1)} %copy-done.5, ...), custom_call_target="tpu_custom_call" | custom-call | flops 1 | bytes 1845000 | tf_op jit(solution)/shard_map/ffn_in/pallas_call | solution.py:492
  116.8 14.3 %ffn_out.1 = (bf16[512,768]{1,0:T(8,128)(2,1)}, bf16[512,768]{1,0:T(8,128)(2,1)}, f32[8,1024]{1,0:T(8,128)}, bf16[768,1536]{1,0:T(8,128)(2,1)}) custom-call(s32[8]{0:T(128)} %pad_add_fusion.s_ref, f32[1024,1536]{1,0:T(8,128)} %get-tuple-element.128.a_ref, f32[8,1024]{1,0:T(8,128)} %get-tuple-element.129.st_ref, f32[8,1024]{1,0:T(8,128)} %copy-done.26, ...), custom_call_target="tpu_custom_call" | custom-call | flops 1 | bytes 1845000 | tf_op jit(solution)/shard_map/ffn_out/pallas_call | solution.py:547
  133.6 20.6 %ffn_back.1 = (bf16[512,768]{1,0:T(8,128)(2,1)}, bf16[512,768]{1,0:T(8,128)(2,1)}, f32[8,1536]{1,0:T(8,128)}, bf16[384,1536]{1,0:T(8,128)(2,1)}, bf16[400,768]{1,0:T(8,128)(2,1)}, /*index=5*/bf16[400,768]{1,0:T(8,128)(2,1)}) custom-call(s32[8]{0:T(128)} %pad_add_fusion.s_ref, f32[1024,1536]{1,0:T(8,128)} %get-tuple-element.128.a_ref, ...), custom_call_target="tpu_custom_call" | custom-call | flops 1 | bytes 2583000 | tf_op jit(solution)/shard_map/ffn_back/pallas_call | solution.py:646
  157.7 7.3 %join_back.1 = (bf16[512,768]{1,0:T(8,128)(2,1)}, f32[512,768]{1,0:T(8,128)}, bf16[512,768]{1,0:T(8,128)(2,1)}, bf16[512,768]{1,0:T(8,128)(2,1)}) custom-call(s32[8]{0:T(128)} %pad_add_fusion.s_ref, bf16[512,768]{1,0:T(8,128)(2,1)} %get-tuple-element.131.b_ref, bf16[512,768]{1,0:T(8,128)(2,1)} %copy-done.15, bf16[512,768]{1,0:T(8,128)(2,1)} %get-tuple-element.136.f_ref, ...), custom_call_target="tpu_custom_call" | custom-call | flops 1 | bytes 1291500 | tf_op jit(solution)/shard_map/join_back/pallas_call | solution.py:392
  165.0 12.9 %attend_back.1 = (bf16[512,768]{1,0:T(8,128)(2,1)}, f32[512,1536]{1,0:T(8,128)}, bf16[512,1536]{1,0:T(8,128)(2,1)}) custom-call(s32[8]{0:T(128)} %pad_add_fusion.s_ref, bf16[512,768]{1,0:T(8,128)(2,1)} %get-tuple-element.114.q_ref, bf16[512,1536]{1,0:T(8,128)(2,1)} %get-tuple-element.116.kv_ref, bf16[512,1536]{1,0:T(8,128)(2,1)} %copy-done.1, ...), custom_call_target="tpu_custom_call" | custom-call | flops 1 | bytes 3690000 | tf_op jit(solution)/shard_map/attend_back/pallas_call | solution.py:317
  183.5 7.0 %collective-permute-done.26.fkv_ref = bf16[512,1536]{1,0:T(8,128)(2,1)S(1)} collective-permute-done((bf16[512,1536]{1,0:T(8,128)(2,1)}, bf16[512,1536]{1,0:T(8,128)(2,1)S(1)}, u32[]{:S(2)}, u32[]{:S(2)}) %collective-permute-start.26) | collective-permute-done | bytes 1572896 | tf_op jit(solution)/shard_map/ppermute | solution.py:926
  191.6 9.9 %project_grads.1 = (bf16[512,2304]{1,0:T(8,128)(2,1)}, bf16[16,24,3072]{2,1,0:T(8,128)(2,1)}, bf16[16,24,3072]{2,1,0:T(8,128)(2,1)}) custom-call(s32[8]{0:T(128)} %pad_add_fusion.s_ref, bf16[512,768]{1,0:T(8,128)(2,1)} %get-tuple-element.141.n_ref, bf16[512,768]{1,0:T(8,128)(2,1)} %get-tuple-element.144.q_ref, f32[512,1536]{1,0:T(8,128)} %get-tuple-element.145.kv_ref, ...), custom_call_target="tpu_custom_call" | custom-call | flops 1 | bytes 2029500 | tf_op jit(solution)/shard_map/project_grads/pallas_call | solution.py:719
  203.2 7.1 %project_back.1 = bf16[512,768]{1,0:T(8,128)(2,1)} custom-call(s32[8]{0:T(128)} %pad_add_fusion.s_ref, bf16[512,2304]{1,0:T(8,128)(2,1)} %get-tuple-element.158.refs_0_, bf16[512,768]{1,0:T(8,128)(2,1)} %bitcast.42, f32[512,768]{1,0:T(8,128)} %get-tuple-element.162.refs_2_, bf16[768,2304]{1,0:T(8,128)(2,1)} %get-tuple-element.163.refs_3_, ...), custom_call_target="tpu_custom_call" | custom-call | flops 1 | bytes 1291500 | tf_op jit(solution)/shard_map/project_back/pallas_call | solution.py:751
  220.8 11.1 %collective-permute-done.30 = bf16[8,24,1536]{2,1,0:T(8,128)(2,1)S(1)} collective-permute-done((bf16[8,24,1536]{2,1,0:T(8,128)(2,1)S(1)}, bf16[8,24,1536]{2,1,0:T(8,128)(2,1)S(1)}, u32[]{:S(2)}, u32[]{:S(2)}) %collective-permute-start.30) | collective-permute-done | bytes 589856 | tf_op jit(solution)/shard_map/ppermute | solution.py:771
  232.7 2.5 collective-permute-start.35
  240.8 4.9 %collective-permute-done.32 = bf16[4,24,1536]{2,1,0:T(8,128)(2,1)} collective-permute-done((bf16[4,24,1536]{2,1,0:T(8,128)(2,1)}, bf16[4,24,1536]{2,1,0:T(8,128)(2,1)}, u32[]{:S(2)}, u32[]{:S(2)}) %collective-permute-start.32) | collective-permute-done | bytes 294944 | tf_op jit(solution)/shard_map/ppermute | solution.py:771
  259.2 5.6 %collective-permute-done.38 = bf16[24,3072]{1,0:T(8,128)(2,1)S(1)} collective-permute-done((bf16[24,3072]{1,0:T(8,128)(2,1)S(1)}, bf16[24,3072]{1,0:T(8,128)(2,1)S(1)}, u32[]{:S(2)}, u32[]{:S(2)}) %collective-permute-start.38) | collective-permute-done | bytes 147488 | tf_op jit(solution)/shard_map/ppermute | solution.py:771
  (207 shorter events, 81.8 us)
Async XLA Ops:
  7.2 96.6 %all-gather.2.cloned.1.call-start = ((), (), s32[]{:S(2)}) async-start(), calls=%async_computation.2 | async-start | bytes 2506752 | tf_op jit(solution)/shard_map/all_gather | solution.py:839
  9.0 11.7 %collective-permute-start.1 = (bf16[24,2560]{1,0:T(8,128)(2,1)S(1)}, bf16[24,2560]{1,0:T(8,128)(2,1)S(1)}, u32[]{:S(2)}, u32[]{:S(2)}) collective-permute-start(bf16[24,2560]{1,0:T(8,128)(2,1)S(1)} %get-tuple-element.236), channel_id=1, source_target_pairs={{0,16},{2,18},{4,20},{6,22},{8,24},{10,26},{12,28},{14,30},{16,0},... | collective-permute-start | bytes 368648 | tf_op jit(solution)/shard_map/ppermute | solution.py:771
  31.1 21.7 %collective-permute-start.6 = (bf16[8,24,1280]{2,1,0:T(8,128)(2,1)S(1)}, bf16[8,24,1280]{2,1,0:T(8,128)(2,1)S(1)}, u32[]{:S(2)}, u32[]{:S(2)}) collective-permute-start(bf16[8,24,1280]{2,1,0:T(8,128)(2,1)S(1)} %pad_maximum_fusion.9), channel_id=1, source_target_pairs={{0,4},{2,6},{4,0},{6,2},{8,12},{10,14},{12,8},{14,10},{16,20},{18,... | collective-permute-start | bytes 1474568 | tf_op jit(solution)/shard_map/ppermute | solution.py:771
  32.7 20.1 %collective-permute-start.5 = (bf16[8,24,1280]{2,1,0:T(8,128)(2,1)S(1)}, bf16[8,24,1280]{2,1,0:T(8,128)(2,1)S(1)}, u32[]{:S(2)}, u32[]{:S(2)}) collective-permute-start(bf16[8,24,1280]{2,1,0:T(8,128)(2,1)S(1)} %pad_maximum_fusion.8), channel_id=1, source_target_pairs={{0,2},{2,0},{4,6},{6,4},{8,10},{10,8},{12,14},{14,12},{16,18},{18,... | collective-permute-start | bytes 1474568 | tf_op jit(solution)/shard_map/ppermute | solution.py:771
  35.6 16.1 %collective-permute-start.8 = (bf16[48,1920]{1,0:T(8,128)(2,1)S(1)}, bf16[48,1920]{1,0:T(8,128)(2,1)S(1)}, u32[]{:S(2)}, u32[]{:S(2)}) collective-permute-start(bf16[48,1920]{1,0:T(8,128)(2,1)S(1)} %maximum_maximum_fusion), channel_id=1, source_target_pairs={{0,16},{2,18},{4,20},{6,22},{8,24},{10,26},{12,28},{14,30},{16,0},... | collective-permute-start | bytes 552968 | tf_op jit(solution)/shard_map/ppermute | solution.py:771
  38.4 13.3 %collective-permute-start.7 = (bf16[48,1920]{1,0:T(8,128)(2,1)S(1)}, bf16[48,1920]{1,0:T(8,128)(2,1)}, u32[]{:S(2)}, u32[]{:S(2)}) collective-permute-start(bf16[48,1920]{1,0:T(8,128)(2,1)S(1)} %maximum_maximum_fusion), channel_id=1, source_target_pairs={{0,8},{2,10},{4,12},{6,14},{8,0},{10,2},{12,4},{14,6},{16,24},{18,... | collective-permute-start | bytes 552968 | tf_op jit(solution)/shard_map/ppermute | solution.py:771
  39.0 139.0 %reduce-scatter.3.cloned.1.call-start = ((), (), s32[]{:S(2)}) async-start(), calls=%async_computation.3 | async-start | bytes 2949120 | tf_op jit(solution)/shard_map/reduce_scatter | solution.py:900
  53.9 11.6 %collective-permute-start.12 = (bf16[4,48,1024]{2,1,0:T(8,128)(2,1)S(1)}, bf16[4,48,1024]{2,1,0:T(8,128)(2,1)S(1)}, u32[]{:S(2)}, u32[]{:S(2)}) collective-permute-start(bf16[4,48,1024]{2,1,0:T(8,128)(2,1)S(1)} %slice.206.refs_0_), channel_id=1, source_target_pairs={{0,2},{2,0},{4,6},{6,4},{8,10},{10,8},{12,14},{14,12},{16,18},{18,... | collective-permute-start | bytes 1179656 | tf_op jit(solution)/shard_map/ppermute | solution.py:771
  68.8 23.6 %collective-permute-start.15 = (bf16[8,48,1024]{2,1,0:T(8,128)(2,1)}, bf16[8,48,1024]{2,1,0:T(8,128)(2,1)}, u32[]{:S(2)}, u32[]{:S(2)}) collective-permute-start(bf16[8,48,1024]{2,1,0:T(8,128)(2,1)} %pad_maximum_fusion.2), channel_id=1, source_target_pairs={{0,4},{2,6},{4,0},{6,2},{8,12},{10,14},{12,8},{14,10},{16,20},{18,... | collective-permute-start | bytes 2359304 | tf_op jit(solution)/shard_map/ppermute | solution.py:771
  70.4 20.6 %collective-permute-start.16 = (bf16[8,48,896]{2,1,0:T(8,128)(2,1)}, bf16[8,48,896]{2,1,0:T(8,128)(2,1)S(1)}, u32[]{:S(2)}, u32[]{:S(2)}) collective-permute-start(bf16[8,48,896]{2,1,0:T(8,128)(2,1)} %pad_maximum_fusion.4), channel_id=1, source_target_pairs={{0,2},{2,0},{4,6},{6,4},{8,10},{10,8},{12,14},{14,12},{16,18},{18,... | collective-permute-start | bytes 2064392 | tf_op jit(solution)/shard_map/ppermute | solution.py:771
  100.9 14.5 %collective-permute-start.20 = (bf16[512,768]{1,0:T(8,128)(2,1)S(1)}, bf16[512,768]{1,0:T(8,128)(2,1)S(1)}, u32[]{:S(2)}, u32[]{:S(2)}) collective-permute-start(bf16[512,768]{1,0:T(8,128)(2,1)S(1)} %bitcast_select_fusion.n_ref.ng_ref.c_ref), channel_id=1, source_target_pairs={{0,1},{1,0},{2,3},{3,2},{4,5},{5,4},{6,7},{7,6},{8,9},{9,8},{10,11... | collective-permute-start | bytes 2359304 | tf_op jit(solution)/shard_map/ppermute | solution.py:767
  131.1 109.7 %reduce-scatter.5.cloned.1.call-start = ((), (), s32[]{:S(2)}) async-start(), calls=%async_computation.4 | async-start | bytes 737280 | tf_op jit(solution)/shard_map/reduce_scatter | solution.py:927
  132.2 24.0 %collective-permute-start.21 = (bf16[512,768]{1,0:T(8,128)(2,1)S(1)}, bf16[512,768]{1,0:T(8,128)(2,1)S(1)}, u32[]{:S(2)}, u32[]{:S(2)}) collective-permute-start(bf16[512,768]{1,0:T(8,128)(2,1)S(1)} %copy-done.33), channel_id=1, source_target_pairs={{0,1},{1,0},{2,3},{3,2},{4,5},{5,4},{6,7},{7,6},{8,9},{9,8},{10,11... | collective-permute-start | bytes 2359304 | tf_op jit(solution)/shard_map/ppermute | solution.py:767
  154.4 23.6 %collective-permute-start.24 = (bf16[400,768]{1,0:T(8,128)(2,1)}, bf16[400,768]{1,0:T(8,128)(2,1)S(1)}, u32[]{:S(2)}, u32[]{:S(2)}) collective-permute-start(bf16[400,768]{1,0:T(8,128)(2,1)} %get-tuple-element.146), channel_id=1, source_target_pairs={{0,2},{2,0},{4,6},{6,4},{8,10},{10,8},{12,14},{14,12},{16,18},{18,... | collective-permute-start | bytes 1843208 | tf_op jit(solution)/shard_map/ppermute | solution.py:771
  155.5 22.4 %collective-permute-start.25 = (bf16[400,768]{1,0:T(8,128)(2,1)}, bf16[400,768]{1,0:T(8,128)(2,1)S(1)}, u32[]{:S(2)}, u32[]{:S(2)}) collective-permute-start(bf16[400,768]{1,0:T(8,128)(2,1)} %get-tuple-element.147), channel_id=1, source_target_pairs={{0,4},{2,6},{4,0},{6,2},{8,12},{10,14},{12,8},{14,10},{16,20},{18,... | collective-permute-start | bytes 1843208 | tf_op jit(solution)/shard_map/ppermute | solution.py:771
  178.9 11.6 %collective-permute-start.26 = (bf16[512,1536]{1,0:T(8,128)(2,1)}, bf16[512,1536]{1,0:T(8,128)(2,1)S(1)}, u32[]{:S(2)}, u32[]{:S(2)}) collective-permute-start(bf16[512,1536]{1,0:T(8,128)(2,1)} %get-tuple-element.150), channel_id=1, source_target_pairs={{1,0},{3,2},{5,4},{7,6},{9,8},{11,10},{13,12},{15,14},{17,16},{19,... | collective-permute-start | bytes 4718600 | tf_op jit(solution)/shard_map/ppermute | solution.py:926
  201.5 10.5 %collective-permute-start.27 = (bf16[16,24,3072]{2,1,0:T(8,128)(2,1)}, bf16[16,24,3072]{2,1,0:T(8,128)(2,1)S(1)}, u32[]{:S(2)}, u32[]{:S(2)}) collective-permute-start(bf16[16,24,3072]{2,1,0:T(8,128)(2,1)} %get-tuple-element.164), channel_id=1, source_target_pairs={{0,1},{1,0},{2,3},{3,2},{4,5},{5,4},{6,7},{7,6},{8,9},{9,8},{10,11... | collective-permute-start | bytes 7077896 | tf_op jit(solution)/shard_map/ppermute | solution.py:767
  217.4 14.5 %collective-permute-start.30 = (bf16[8,24,1536]{2,1,0:T(8,128)(2,1)S(1)}, bf16[8,24,1536]{2,1,0:T(8,128)(2,1)S(1)}, u32[]{:S(2)}, u32[]{:S(2)}) collective-permute-start(bf16[8,24,1536]{2,1,0:T(8,128)(2,1)S(1)} %get-tuple-element.170), channel_id=1, source_target_pairs={{0,2},{2,0},{4,6},{6,4},{8,10},{10,8},{12,14},{14,12},{16,18},{18,... | collective-permute-start | bytes 1769480 | tf_op jit(solution)/shard_map/ppermute | solution.py:771
  218.4 14.3 %collective-permute-start.31 = (bf16[8,24,1536]{2,1,0:T(8,128)(2,1)S(1)}, bf16[8,24,1536]{2,1,0:T(8,128)(2,1)S(1)}, u32[]{:S(2)}, u32[]{:S(2)}) collective-permute-start(bf16[8,24,1536]{2,1,0:T(8,128)(2,1)S(1)} %get-tuple-element.171), channel_id=1, source_target_pairs={{0,4},{2,6},{4,0},{6,2},{8,12},{10,14},{12,8},{14,10},{16,20},{18,... | collective-permute-start | bytes 1769480 | tf_op jit(solution)/shard_map/ppermute | solution.py:771
  232.7 19.4 %collective-permute-start.35 = (bf16[64,1536]{1,0:T(8,128)(2,1)}, bf16[64,1536]{1,0:T(8,128)(2,1)}, u32[]{:S(2)}, u32[]{:S(2)}) collective-permute-start(bf16[64,1536]{1,0:T(8,128)(2,1)} %get-tuple-element.187), channel_id=1, source_target_pairs={{0,8},{2,10},{4,12},{6,14},{8,0},{10,2},{12,4},{14,6},{16,24},{18,... | collective-permute-start | bytes 589832 | tf_op jit(solution)/shard_map/ppermute | solution.py:771
  235.2 19.4 %collective-permute-start.36 = (bf16[64,1536]{1,0:T(8,128)(2,1)}, bf16[64,1536]{1,0:T(8,128)(2,1)}, u32[]{:S(2)}, u32[]{:S(2)}) collective-permute-start(bf16[64,1536]{1,0:T(8,128)(2,1)} %get-tuple-element.188), channel_id=1, source_target_pairs={{0,16},{2,18},{4,20},{6,22},{8,24},{10,26},{12,28},{14,30},{16,0},... | collective-permute-start | bytes 589832 | tf_op jit(solution)/shard_map/ppermute | solution.py:771
  236.7 17.9 %collective-permute-start.37 = (bf16[64,1536]{1,0:T(8,128)(2,1)}, bf16[64,1536]{1,0:T(8,128)(2,1)}, u32[]{:S(2)}, u32[]{:S(2)}) collective-permute-start(bf16[64,1536]{1,0:T(8,128)(2,1)} %get-tuple-element.189), channel_id=1, source_target_pairs={{0,24},{2,26},{4,28},{6,30},{8,16},{10,18},{12,20},{14,22},{16,8},... | collective-permute-start | bytes 589832 | tf_op jit(solution)/shard_map/ppermute | solution.py:771
  250.1 14.7 %collective-permute-start.38 = (bf16[24,3072]{1,0:T(8,128)(2,1)S(1)}, bf16[24,3072]{1,0:T(8,128)(2,1)S(1)}, u32[]{:S(2)}, u32[]{:S(2)}) collective-permute-start(bf16[24,3072]{1,0:T(8,128)(2,1)S(1)} %get-tuple-element.191), channel_id=1, source_target_pairs={{0,16},{2,18},{4,20},{6,22},{8,24},{10,26},{12,28},{14,30},{16,0},... | collective-permute-start | bytes 442376 | tf_op jit(solution)/shard_map/ppermute | solution.py:771
  252.1 12.7 %collective-permute-start.39 = (bf16[24,3072]{1,0:T(8,128)(2,1)S(1)}, bf16[24,3072]{1,0:T(8,128)(2,1)S(1)}, u32[]{:S(2)}, u32[]{:S(2)}) collective-permute-start(bf16[24,3072]{1,0:T(8,128)(2,1)S(1)} %get-tuple-element.192), channel_id=1, source_target_pairs={{0,24},{2,26},{4,28},{6,30},{8,16},{10,18},{12,20},{14,22},{16,8},... | collective-permute-start | bytes 442376 | tf_op jit(solution)/shard_map/ppermute | solution.py:771
  (54 other events, 370.9 us)
Sparse Core Ops, SparseCore 0:
  39.1 64.5 all-gather.1
  131.2 44.1 reduce-scatter.2
  203.4 22.2 reduce-scatter.4
where the time goes:
time: 276 us; the launch traced here: 275 us
  Pallas kernels  107 us (39%)
  waiting for transfers between devices  74.5 us (27%)
  starting transfers between devices  43.2 us (16%)
  other arithmetic  19.7 us (7%)
  local copies, waits for them, and re-layouts  15.6 us (6%)
  between operations  15 us (5%)
    ppermute x28, waiting for transfers between devices, exchange(): return lax.ppermute(array, CHIPS, [(i, i ^ mask) for i in range(chips)])  60.6 us
    ppermute x28, starting transfers between devices, exchange(): return lax.ppermute(array, CHIPS, [(i, i ^ mask) for i in range(chips)])  36.9 us
    pallas_call x1, Pallas kernels, ffn_back(): call(body, 'ffn_back', (shaped((rows, width), BF16), shaped((rows, width)...  20.6 us
    pallas_call x1, Pallas kernels, ffn_out(): call(body, 'ffn_out', (shaped((rows, width), BF16), shaped((rows, width),...  14.3 us
    pallas_call x1, Pallas kernels, attend_back(): call(body, 'attend_back', (shaped((rows, width), BF16), shaped((rows, 2 *...  12.9 us
    pallas_call x1, Pallas kernels, attend(): call(body, 'attend', (shaped((rows, width), F32), shaped((rows, width), F...  10.9 us
    unnamed x68, local copies, waits for them, and re-layouts  10.4 us
    pallas_call x1, Pallas kernels, ffn_in(): call(body, 'ffn_in', (shaped((2 * rows, units), F32), shaped((2 * rows, u...  9.98 us
  transfers between devices with their start and end apart: 44, of which 24 were waited for; matrix products, arithmetic and copies ran while one was open for 7% of the time, Pallas kernels for 30%

commit v1 on v0

--- a/solution.py
+++ b/solution.py
@@ -27,6 +27,7 @@
     "attend_back": 20,
     "project_grads": 11,
     "project_back": 7,
+    "finish": 2,
 }
 
 
@@ -207,8 +208,10 @@
                         mixed = mixed + mm(beyond.astype(BF16), fkv_ref[:, PAIR : 2 * PAIR])
                     sums.append(mixed / total)
                     logs.append(jnp.broadcast_to(highest + jnp.log(total), (tile, PAIR)))
-                o_ref[t * tile : end] = jnp.where(lane_of(0), sums[0], sums[1])
-                l_ref[t * tile : end] = jnp.where(lane_of(0), logs[0], logs[1])
+                o_ref[t * tile : end] = jnp.where(lane_of(0), sums[0], sums[1]).astype(BF16)
+                turned = jnp.transpose(jnp.where(lane_of(0), logs[0], logs[1]))
+                upper = lax.broadcasted_iota(jnp.int32, (8, tile), 0) < 4
+                l_ref[0, :, t * tile : end] = jnp.where(upper, turned[0:8], turned[HEAD_DIM : HEAD_DIM + 8])
 
         @pl.when(s_ref[1] == 0)
         def _():
@@ -220,13 +223,14 @@
 
     spec = pl.BlockSpec((rows, PAIR), lambda i, s: (0, i))
     both = pl.BlockSpec((rows, 2 * PAIR), lambda i, s: (0, i))
+    log_spec = pl.BlockSpec((1, 8, rows), lambda i, s: (i, 0, 0))
     return call(
         body,
         "attend",
-        (shaped((rows, width), F32), shaped((rows, width), F32)),
+        (shaped((rows, width), BF16), shaped((pairs, 8, rows), F32)),
         (pairs,),
         [spec, both, both],
-        (spec, spec),
+        (spec, log_spec),
     )(scalars, queries, near, far_side)
 
 
@@ -245,7 +249,6 @@
         def run(far):
             query = q_ref[...] * jnp.asarray(0.125, BF16)
             grad = d_ref[...]
-            log_rows = jnp.transpose(l_ref[...])
             picker = jnp.where(
                 lax.broadcasted_iota(jnp.int32, (8, PAIR), 1) // HEAD_DIM
                 == lax.broadcasted_iota(jnp.int32, (8, PAIR), 0),
@@ -254,7 +257,7 @@
             ).astype(F32)
             dots = lax.dot_general(
                 picker,
-                grad.astype(F32) * o_ref[...],
+                grad.astype(F32) * o_ref[...].astype(F32),
                 (((1,), (1,)), ((), ())),
                 precision=lax.Precision.HIGHEST,
                 preferred_element_type=F32,
@@ -287,7 +290,7 @@
                     if masked:
                         scores = jnp.where(allowed, scores, MASKED)
                     base = head * HEAD_DIM
-                    probs = jnp.exp(scores - log_rows[base : base + 1, low:rows])
+                    probs = jnp.exp(scores - l_ref[0, 4 * head : 4 * head + 1, low:rows])
                     prob_grad = mm_tail(value, mine_grad)
                     score_grad = (probs * (prob_grad - dots[head : head + 1, low:rows])).astype(BF16)
                     vgrads.append(mm(probs.astype(BF16), grad[low:rows]))
@@ -314,12 +317,13 @@
     both = pl.BlockSpec((rows, 2 * PAIR), lambda i, s: (0, i + first))
     own = pl.BlockSpec((rows, PAIR), lambda i, s: (0, i))
     own_both = pl.BlockSpec((rows, 2 * PAIR), lambda i, s: (0, i))
+    log_spec = pl.BlockSpec((1, 8, rows), lambda i, s: (i + first, 0, 0))
     return call(
         body,
         "attend_back",
-        (shaped((rows, width), BF16), shaped((rows, 2 * width), F32), shaped((rows, 2 * width), BF16)),
+        (shaped((rows, width), BF16), shaped((rows, 2 * width), BF16), shaped((rows, 2 * width), BF16)),
         (pairs,),
-        [spec, both, both, spec, spec, spec],
+        [spec, both, both, spec, spec, log_spec],
         (own, own_both, own_both),
     )(scalars, queries, near, far_side, grads, attended, logs)
 
@@ -339,7 +343,7 @@
             else:
                 put_blocks(s_ref, pieces, places, w_ref, 0, width)
 
-        hat, _ = norm_stats(a_ref[...])
+        hat, _ = norm_stats(a_ref[...].astype(F32))
         low = (hat * g_ref[1:2, :]).astype(BF16)
         sub_ref[...] = low
         middle = x_ref[...].astype(F32) + mm(low, w_ref[...])
@@ -385,7 +389,7 @@
         low = middle_grad.astype(BF16)
         ml_ref[...] = low
         sub_grad = mm_tail(low, w_ref[...])
-        hat, inverse = norm_stats(a_ref[...])
+        hat, inverse = norm_stats(a_ref[...].astype(F32))
         ag_ref[...] = norm_back(sub_grad, g_ref[1:2, :], hat, inverse).astype(BF16)
 
     spec = rows_of((tile, width))
@@ -480,7 +484,7 @@
             cdf = 0.5 * (1.0 + lax.erf(pre * 0.7071067811865476))
             pdf = 0.3989422804014327 * jnp.exp(-0.5 * pre * pre)
             act = pre * cdf
-            act_ref[:, at : at + chunk] = act
+            act_ref[:, at : at + chunk] = act.astype(BF16)
             slope_ref[:, at : at + chunk] = (cdf + pre * pdf).astype(slope_ref.dtype)
             sums = sums + fold(act)
             squares = squares + fold(act * act)
@@ -493,7 +497,7 @@
         body,
         "ffn_in",
         (
-            shaped((2 * rows, units), F32),
+            shaped((2 * rows, units), BF16),
             shaped((2 * rows, units), BF16),
             shaped((8, 2 * rows), F32),
             shaped((width, units), BF16),
@@ -523,7 +527,7 @@
         center, inverse = unit_norm(st_ref[...], fs_ref[...], 2 * units)
         at_row = pl.multiple_of(step * tile, tile)
         for at in range(0, units, chunk):
-            hat = (a_ref[:, at : at + chunk] - center) * inverse
+            hat = (a_ref[:, at : at + chunk].astype(F32) - center) * inverse
             stash[pl.ds(at_row, tile), at : at + chunk] = (hat * g_ref[:, at : at + chunk]).astype(BF16)
         branch = mm_tail(stash[pl.ds(at_row, tile), :], weight[...])
         to_side(step < steps, b_ref, fb_ref, branch)
@@ -598,7 +602,7 @@
 
         for at in range(0, units, chunk):
             normed = mm(grad, wo_ref[0, :, at : at + chunk])
-            hat = (a_ref[:, at : at + chunk] - center) * inverse
+            hat = (a_ref[:, at : at + chunk].astype(F32) - center) * inverse
             fourth[:, at : at + chunk] += jnp.sum((normed * hat).reshape(tile // 8, 8, chunk), 0)
             act_grad = inverse * (normed * g_ref[:, at : at + chunk] - first - hat * second)
             stash[pl.ds(at_row, tile), at : at + chunk] = (
@@ -691,7 +695,7 @@
         low_ref, *outs, grad_ref = refs
         me, core = s_ref[0], s_ref[1]
         near = core == 0
-        both = kv_ref[...] + jnp.where(near, fkv_ref[...].astype(F32), 0.0)
+        both = kv_ref[...].astype(F32) + jnp.where(near, fkv_ref[...].astype(F32), 0.0)
         low_ref[:, 0:cols] = q_ref[...]
         for pair in range(pairs):
             for which in range(2):
@@ -705,27 +709,80 @@
         if blocks == 1:
             outs[0][0] = grad_ref[...].astype(BF16)
             return
-        for side, out in ((0, outs[0]), (1, outs[1])):
+        for side in range(2):
             owner = core if side == 0 else 1 - core
+            later, *firsts = outs[3 * side : 3 * side + 3]
             for block in range(blocks):
                 position = block ^ me
                 row = pl.multiple_of(block * depth + owner * own, 8)
                 for order, start, end in parts:
                     slot = slot_of(position, order, blocks)
-                    out[slot, :, start:end] = grad_ref[pl.ds(row, own), start:end].astype(BF16)
+                    low = grad_ref[pl.ds(row, own), start:end].astype(BF16)
+
+                    @pl.when(slot < blocks // 2)
+                    def _():
+                        later[slot, :, start:end] = low
+
+                    @pl.when(slot >= blocks // 2)
+                    def _():
+                        firsts[order][slot - blocks // 2] = low
 
     more = list(extra) if extra else []
-    pieces = 1 if blocks == 1 else 2
+    shapes = [shape]
+    if blocks > 1:
+        shapes = [(blocks // 2, own, total)] + [(blocks // 2, own, end - start) for _, start, end in parts]
+        shapes = shapes * 2
     return call(
         body,
         "project_grads",
-        (shaped((rows, 3 * cols), BF16),) + (shaped(shape, BF16),) * pieces,
+        (shaped((rows, 3 * cols), BF16),) + tuple(shaped(each, BF16) for each in shapes),
         (1,),
         [whole((rows, width)), whole((rows, cols)), whole((rows, 2 * cols)), whole((rows, 2 * cols))]
         + [whole((rows, width))] * len(more),
-        (whole((rows, 3 * cols)),) + (whole(shape),) * pieces,
+        (whole((rows, 3 * cols)),) + tuple(whole(each) for each in shapes),
         scratch=[pltpu.VMEM((width, total), F32)],
     )(scalars, normed, dq, dkv, far_dkv, *more)
+
+
+def finish(pieces, query_key, value_proj, output_proj, gains, scalars):
+    rows, columns = pieces[0].shape
+    width = columns // 4
+
+    def body(s_ref, *refs):
+        ins = refs[: len(pieces)]
+        qk_ref, v_ref, o_ref, one_ref, two_ref, qk_out, v_out, o_out, one_out, two_out = refs[len(pieces) :]
+
+        def total(start, end):
+            value = ins[0][:, start:end].astype(F32)
+            for piece in ins[1:]:
+                value = value + piece[:, start:end].astype(F32)
+            return value
+
+        qk, v, o = total(0, 2 * width), total(2 * width, 3 * width), total(3 * width, columns)
+        qk_out[...] = qk
+        v_out[...] = v
+        o_out[...] = o
+        one = fold(qk * qk_ref[...].astype(F32)) + fold(v * v_ref[...].astype(F32))
+        two = fold(o * o_ref[...].astype(F32))
+        for sums, gain_ref, out in ((one, one_ref, one_out), (two, two_ref, two_out)):
+            turned = lax.dot_general(
+                jnp.ones((8, 128), F32),
+                sums,
+                (((1,), (1,)), ((), ())),
+                precision=lax.Precision.HIGHEST,
+                preferred_element_type=F32,
+            )
+            out[...] = turned[0:1] / gain_ref[...]
+
+    shapes = ((rows, 2 * width), (rows, width), (rows, width), (1, rows), (1, rows))
+    return call(
+        body,
+        "finish",
+        tuple(shaped(shape, F32) for shape in shapes),
+        (1,),
+        [whole(p.shape) for p in pieces] + [whole(shape) for shape in shapes],
+        tuple(whole(shape) for shape in shapes),
+    )(scalars, *pieces, query_key, value_proj, output_proj, *gains)
 
 
 def project_back(lows, inputs, middle_grad, weights, gains, scalars):
@@ -934,24 +991,24 @@
         ]
         far_dkv, sent[0], sent[1], in_kept = barrier((far_dkv, sent[0], sent[1], in_kept))
         got = [exchange(sent[0], 2, chips), exchange(sent[1], 1, chips)]
-        low, keep, send = project_grads(
+        low, keep, keep_one, keep_two, send, send_one, send_two = project_grads(
             normed, dq, dkv, far_dkv, extra, ((0, 0, cut), (1, cut, columns)), scalars, chips
         )
-        middle_grad, keep, send = barrier((middle_grad, keep, send))
-        other = other_core(send)
+        middle_grad, send, send_one, send_two = barrier((middle_grad, send, send_one, send_two))
+        other_one, other_two, other = other_core(send_one), other_core(send_two), other_core(send)
         inputs_grad = project_back([low], series, middle_grad, weights, gains, scalars)
-        inputs_grad, other, got[0], got[1] = barrier((inputs_grad, other, got[0], got[1]))
-        upper_one = add_low(keep[middle:, :, :cut], other[middle:, :, :cut])
-        upper_two = add_low(keep[middle:, :, cut:], other[middle:, :, cut:])
+        inputs_grad, other_one, other_two, other, got[0], got[1] = barrier(
+            (inputs_grad, other_one, other_two, other, got[0], got[1])
+        )
+        upper_one, upper_two = add_low(keep_one, other_one), add_low(keep_two, other_two)
         upper_one, upper_two = barrier((upper_one, upper_two))
         got_one, got_two = exchange(upper_one, 1, chips), exchange(upper_two, 2, chips)
         in_held, fourth = add_parts(in_kept, fourth, got, 0, count // 2)
         in_held = in_held.reshape(chips // 4, depth, units)
         sends = barrier(tuple(outer_sends(in_held, fourth)))
-        got_one, got_two, *sends = barrier((got_one, got_two, *sends))
         in_got = exchange_outer(sends, chips)
-        sent_first = sum_low(keep[lower:middle, :, :cut], other[lower:middle, :, :cut], got_one[lower:])
-        sent_second = sum_low(keep[lower:middle, :, cut:], other[lower:middle, :, cut:], got_two[lower:])
+        sent_first = sum_low(keep[lower:, :, :cut], other[lower:, :, :cut], got_one[lower:])
+        sent_second = sum_low(keep[lower:, :, cut:], other[lower:, :, cut:], got_two[lower:])
         sent_first, sent_second = barrier((sent_first, sent_second))
         got_first, got_second = exchange(sent_first, 2, chips), exchange(sent_second, 1, chips)
         kept = sum_low(keep[:lower], other[:lower], jnp.concatenate([got_one[:lower], got_two[:lower]], -1))
@@ -968,10 +1025,7 @@
         third_part = jnp.broadcast_to(third_part, (depth, 128))
         third_part = third_part + other_core(third_part)
         *both_got, third_part = barrier((*both_got, third_part))
-        total = both[0].astype(F32)
-        for piece in both_got:
-            total = total + piece.astype(F32)
-        large = total
+        last = [both[0], *both_got]
     else:
         dq, dkv, far_dkv = attend_back(queries, near_kv, far_kv, attended_low, attended, logs, scalars, 0, pairs)
         far_dkv = lax.ppermute(far_dkv, CORES, [(1, 0)])
@@ -981,16 +1035,16 @@
         inputs_grad = project_back([low], series, middle_grad, weights, gains, scalars)
         in_payload = lax.psum_scatter(in_payload[0], CHIPS, scatter_dimension=0, tiled=True).astype(F32)
         fourth = lax.psum(fourth_term[0:1], CHIPS)
-        large = lax.dynamic_slice_in_dim(mine, core * (depth // 2), depth // 2, 0)
+        last = [lax.dynamic_slice_in_dim(mine, core * (depth // 2), depth // 2, 0)]
         third_part = lax.psum(jnp.sum(hidden_in.astype(F32) * in_payload, 1, keepdims=True), CORES)
     hidden_out_sum = out_payload.astype(F32).T
     hidden_in_sum = in_payload
     third_sum = lax.dynamic_slice_in_dim(third_part[:, 0], core * (depth // 2), depth // 2) / third_gain.astype(F32)
-    qk_sum, value_sum, output_sum = large[:, : 2 * width], large[:, 2 * width : 3 * width], large[:, 3 * width :]
-    first_sum = (
-        jnp.sum(query_key.astype(F32) * qk_sum, 1) + jnp.sum(value_proj.astype(F32) * value_sum, 1)
-    ) / first_gain.astype(F32)
-    second_sum = jnp.sum(output_proj.astype(F32) * output_sum, 1) / second_gain.astype(F32)
+    gain_rows = [gain.astype(F32)[None, :] for gain in (first_gain, second_gain)]
+    qk_sum, value_sum, output_sum, first_sum, second_sum = finish(
+        last, query_key, value_proj, output_proj, gain_rows, scalars
+    )
+    first_sum, second_sum = first_sum[0], second_sum[0]
     return (
         outputs[None],
         inputs_grad[None],

time: 276 us -> 267 us (0.967)
  waiting for transfers between devices: 74.5 us -> 65.6 us
  Pallas kernels: 107 us -> 110 us
  local copies, waits for them, and re-layouts: 15.6 us -> 12.8 us
    ppermute x28, waiting for transfers between devices: 60.6 us -> 50.9 us  [exchange(): return lax.ppermute(array, CHIPS, [(i, i ^ mask) for i in range(chips)])]
    pallas_call x3 -> x4, Pallas kernels: 30.8 us -> 35.1 us  [the longest x1 11.6 us: attend(): call(body, 'attend', (shaped((rows, width), BF16), shaped((pairs, 8, rows...]
    unnamed x68 -> x76, local copies, waits for them, and re-layouts: 10.4 us -> 9.45 us
  transfers between devices with their start and end apart: 44 -> 46, of which waited for: 24 -> 24; matrix products, arithmetic and copies ran while one was open for 7% -> 6% of each run, Pallas kernels for 30% -> 31%
where the time goes in v1:
time: 267 us; the launch traced here: 266 us
  Pallas kernels  110 us (41%)
  waiting for transfers between devices  65.6 us (25%)
  starting transfers between devices  44.6 us (17%)
  other arithmetic  17.8 us (7%)
  between operations  15 us (6%)
  local copies, waits for them, and re-layouts  12.8 us (5%)
    ppermute x28, waiting for transfers between devices, exchange(): return lax.ppermute(array, CHIPS, [(i, i ^ mask) for i in range(chips)])  50.9 us
    ppermute x28, starting transfers between devices, exchange(): return lax.ppermute(array, CHIPS, [(i, i ^ mask) for i in range(chips)])  38 us
    pallas_call x1, Pallas kernels, ffn_back(): call(body, 'ffn_back', (shaped((rows, width), BF16), shaped((rows, width)...  20.4 us
    pallas_call x1, Pallas kernels, ffn_out(): call(body, 'ffn_out', (shaped((rows, width), BF16), shaped((rows, width),...  14 us
    pallas_call x1, Pallas kernels, attend_back(): call(body, 'attend_back', (shaped((rows, width), BF16), shaped((rows, 2 *...  12.8 us
    pallas_call x1, Pallas kernels, attend(): call(body, 'attend', (shaped((rows, width), BF16), shaped((pairs, 8, rows...  11.6 us
    pallas_call x1, Pallas kernels, project_grads(): call(body, 'project_grads', (shaped((rows, 3 * cols), BF16),) + tuple((sh...  10.5 us
    pallas_call x1, Pallas kernels, ffn_in(): call(body, 'ffn_in', (shaped((2 * rows, units), BF16), shaped((2 * rows,...  10.4 us
  transfers between devices with their start and end apart: 46, of which 24 were waited for; matrix products, arithmetic and copies ran while one was open for 6% of the time, Pallas kernels for 31%

profile of v1, /device:TPU:0, one launch (start us, length us, event | category | flops | bytes accessed | tf_op | source)
XLA Modules:
  0.0 265.7 jit_solution(13415855498614416385)
XLA Ops:
  9.0 4.1 %collective-permute-start.1 = (bf16[24,2560]{1,0:T(8,128)(2,1)S(1)}, bf16[24,2560]{1,0:T(8,128)(2,1)S(1)}, u32[]{:S(2)}, u32[]{:S(2)}) collective-permute-start(bf16[24,2560]{1,0:T(8,128)(2,1)S(1)} %get-tuple-element.241), channel_id=1, source_target_pairs={{0,16},{2,18},{4,20},{6,22},{8,24},{10,26},{12,28},{14,30},{16,0},... | collective-permute-start | bytes 368648 | tf_op jit(solution)/shard_map/ppermute | solution.py:828
  16.3 4.4 %collective-permute-done.1 = bf16[24,2560]{1,0:T(8,128)(2,1)S(1)} collective-permute-done((bf16[24,2560]{1,0:T(8,128)(2,1)S(1)}, bf16[24,2560]{1,0:T(8,128)(2,1)S(1)}, u32[]{:S(2)}, u32[]{:S(2)}) %collective-permute-start.1) | collective-permute-done | bytes 122912 | tf_op jit(solution)/shard_map/ppermute | solution.py:828
  26.0 3.8 %collective-permute-done.4 = bf16[4,24,1280]{2,1,0:T(8,128)(2,1)S(1)} collective-permute-done((bf16[4,24,1280]{2,1,0:T(8,128)(2,1)S(1)}, bf16[4,24,1280]{2,1,0:T(8,128)(2,1)S(1)}, u32[]{:S(2)}, u32[]{:S(2)}) %collective-permute-start.4) | collective-permute-done | bytes 245792 | tf_op jit(solution)/shard_map/ppermute | solution.py:828
  35.6 2.8 %collective-permute-start.8 = (bf16[48,1920]{1,0:T(8,128)(2,1)S(1)}, bf16[48,1920]{1,0:T(8,128)(2,1)S(1)}, u32[]{:S(2)}, u32[]{:S(2)}) collective-permute-start(bf16[48,1920]{1,0:T(8,128)(2,1)S(1)} %maximum_maximum_fusion), channel_id=1, source_target_pairs={{0,16},{2,18},{4,20},{6,22},{8,24},{10,26},{12,28},{14,30},{16,0},... | collective-permute-start | bytes 552968 | tf_op jit(solution)/shard_map/ppermute | solution.py:828
  41.3 10.5 %collective-permute-done.8 = bf16[48,1920]{1,0:T(8,128)(2,1)S(1)} collective-permute-done((bf16[48,1920]{1,0:T(8,128)(2,1)S(1)}, bf16[48,1920]{1,0:T(8,128)(2,1)S(1)}, u32[]{:S(2)}, u32[]{:S(2)}) %collective-permute-start.8) | collective-permute-done | bytes 184352 | tf_op jit(solution)/shard_map/ppermute | solution.py:828
  57.2 8.2 %project.1 = (bf16[512,768]{1,0:T(8,128)(2,1)}, bf16[512,1536]{1,0:T(8,128)(2,1)}, bf16[512,768]{1,0:T(8,128)(2,1)}, bf16[768,2304]{1,0:T(8,128)(2,1)}, f32[8,768]{1,0:T(8,128)}) custom-call(s32[8]{0:T(128)} %pad_add_fusion.s_ref, bf16[512,768]{1,0:T(8,128)(2,1)} %bitcast.45, bf16[16,24,1280]{2,1,0:T(8,128)(2,1)} %copy-done.3, ...), custom_call_target="tpu_custom_call" | custom-call | flops 1 | bytes 1476000 | tf_op jit(solution)/shard_map/project/pallas_call | solution.py:153
  72.5 11.6 %attend.1 = (bf16[512,768]{1,0:T(8,128)(2,1)}, f32[6,8,512]{2,1,0:T(8,128)}) custom-call(s32[8]{0:T(128)} %pad_add_fusion.s_ref, bf16[512,768]{1,0:T(8,128)(2,1)} %get-tuple-element.121.q_ref, bf16[512,1536]{1,0:T(8,128)(2,1)} %get-tuple-element.123.kv_ref, bf16[512,1536]{1,0:T(8,128)(2,1)} %copy-done.1), custom_call_target="tpu_custom_call" | custom-call | flops 1 | bytes 2767500 | tf_op jit(solution)/shard_map/attend/pallas_call | solution.py:227
  84.1 6.6 %collective-permute-done.16.refs_5_ = bf16[8,48,896]{2,1,0:T(8,128)(2,1)S(1)} collective-permute-done((bf16[8,48,896]{2,1,0:T(8,128)(2,1)}, bf16[8,48,896]{2,1,0:T(8,128)(2,1)S(1)}, u32[]{:S(2)}, u32[]{:S(2)}) %collective-permute-start.16) | collective-permute-done | bytes 688160 | tf_op jit(solution)/shard_map/ppermute | solution.py:828
  95.2 5.1 %join.1 = (bf16[512,768]{1,0:T(8,128)(2,1)}, f32[512,768]{1,0:T(8,128)}, bf16[512,768]{1,0:T(8,128)(2,1)}, bf16[768,768]{1,0:T(8,128)(2,1)}) custom-call(s32[8]{0:T(128)} %pad_add_fusion.s_ref, bf16[512,768]{1,0:T(8,128)(2,1)} %get-tuple-element.129.a_ref.o_ref, bf16[512,768]{1,0:T(8,128)(2,1)} %bitcast.46, f32[8,768]{1,0:T(8,128)} %get-tuple-element.130.g_ref.refs_4_, ...), custom_call_target="tpu_custom_call" | custom-call | flops 1 | bytes 922500 | tf_op jit(solution)/shard_map/join/pallas_call | solution.py:355
  101.0 2.7 %all-gather.2.cloned.1.call-done = bf16[768,1536]{1,0:T(8,128)(2,1)} async-done(((bf16[48,1536]{1,0:T(8,128)(2,1)}), bf16[768,1536]{1,0:T(8,128)(2,1)}) %all-gather.2.cloned.1.call-update) | async-done | bytes 2359312 | tf_op jit(solution)/shard_map/all_gather | solution.py:896
  104.6 10.4 %ffn_in.1 = (bf16[1024,1536]{1,0:T(8,128)(2,1)}, bf16[1024,1536]{1,0:T(8,128)(2,1)}, f32[8,1024]{1,0:T(8,128)}, bf16[768,1536]{1,0:T(8,128)(2,1)}) custom-call(s32[8]{0:T(128)} %pad_add_fusion.s_ref, bf16[512,768]{1,0:T(8,128)(2,1)} %get-tuple-element.132.n_ref, bf16[512,768]{1,0:T(8,128)(2,1)} %copy-done.6, bf16[4,48,1024]{2,1,0:T(8,128)(2,1)} %copy-done.5, ...), custom_call_target="tpu_custom_call" | custom-call | flops 1 | bytes 1845000 | tf_op jit(solution)/shard_map/ffn_in/pallas_call | solution.py:496
  117.1 14.0 %ffn_out.1 = (bf16[512,768]{1,0:T(8,128)(2,1)}, bf16[512,768]{1,0:T(8,128)(2,1)}, f32[8,1024]{1,0:T(8,128)}, bf16[768,1536]{1,0:T(8,128)(2,1)}) custom-call(s32[8]{0:T(128)} %pad_add_fusion.s_ref, bf16[1024,1536]{1,0:T(8,128)(2,1)} %get-tuple-element.135.a_ref, f32[8,1024]{1,0:T(8,128)} %get-tuple-element.136.st_ref, f32[8,1024]{1,0:T(8,128)} %copy-done.30, ...), custom_call_target="tpu_custom_call" | custom-call | flops 1 | bytes 1845000 | tf_op jit(solution)/shard_map/ffn_out/pallas_call | solution.py:551
  133.6 20.4 %ffn_back.1 = (bf16[512,768]{1,0:T(8,128)(2,1)}, bf16[512,768]{1,0:T(8,128)(2,1)}, f32[8,1536]{1,0:T(8,128)}, bf16[384,1536]{1,0:T(8,128)(2,1)}, bf16[400,768]{1,0:T(8,128)(2,1)}, /*index=5*/bf16[400,768]{1,0:T(8,128)(2,1)}) custom-call(s32[8]{0:T(128)} %pad_add_fusion.s_ref, bf16[1024,1536]{1,0:T(8,128)(2,1)} %get-tuple-element.135.a_ref, ...), custom_call_target="tpu_custom_call" | custom-call | flops 1 | bytes 2583000 | tf_op jit(solution)/shard_map/ffn_back/pallas_call | solution.py:650
  157.5 7.3 %join_back.1 = (bf16[512,768]{1,0:T(8,128)(2,1)}, f32[512,768]{1,0:T(8,128)}, bf16[512,768]{1,0:T(8,128)(2,1)}, bf16[512,768]{1,0:T(8,128)(2,1)}) custom-call(s32[8]{0:T(128)} %pad_add_fusion.s_ref, bf16[512,768]{1,0:T(8,128)(2,1)} %get-tuple-element.138.b_ref, bf16[512,768]{1,0:T(8,128)(2,1)} %copy-done.17, bf16[512,768]{1,0:T(8,128)(2,1)} %get-tuple-element.143.f_ref, ...), custom_call_target="tpu_custom_call" | custom-call | flops 1 | bytes 1291500 | tf_op jit(solution)/shard_map/join_back/pallas_call | solution.py:396
  164.8 12.8 %attend_back.1 = (bf16[512,768]{1,0:T(8,128)(2,1)}, bf16[512,1536]{1,0:T(8,128)(2,1)}, bf16[512,1536]{1,0:T(8,128)(2,1)}) custom-call(s32[8]{0:T(128)} %pad_add_fusion.s_ref, bf16[512,768]{1,0:T(8,128)(2,1)} %get-tuple-element.121.q_ref, bf16[512,1536]{1,0:T(8,128)(2,1)} %get-tuple-element.123.kv_ref, bf16[512,1536]{1,0:T(8,128)(2,1)} %copy-done.1, ...), custom_call_target="tpu_custom_call" | custom-call | flops 1 | bytes 3690000 | tf_op jit(solution)/shard_map/attend_back/pallas_call | solution.py:321
  182.6 7.4 %collective-permute-done.26.fkv_ref = bf16[512,1536]{1,0:T(8,128)(2,1)S(1)} collective-permute-done((bf16[512,1536]{1,0:T(8,128)(2,1)}, bf16[512,1536]{1,0:T(8,128)(2,1)S(1)}, u32[]{:S(2)}, u32[]{:S(2)}) %collective-permute-start.26) | collective-permute-done | bytes 1572896 | tf_op jit(solution)/shard_map/ppermute | solution.py:983
  191.2 10.5 %project_grads.1 = (bf16[512,2304]{1,0:T(8,128)(2,1)}, bf16[8,24,3072]{2,1,0:T(8,128)(2,1)}, bf16[8,24,1536]{2,1,0:T(8,128)(2,1)}, bf16[8,24,1536]{2,1,0:T(8,128...) custom-call(s32[8]{0:T(128)} %pad_add_fusion.s_ref, ...), custom_call_target="tpu_custom_call" | custom-call | flops 1 | bytes 2029500 | tf_op jit(solution)/shard_map/project_grads/pallas_call | solution.py:735
  204.2 7.1 %project_back.1 = bf16[512,768]{1,0:T(8,128)(2,1)} custom-call(s32[8]{0:T(128)} %pad_add_fusion.s_ref, bf16[512,2304]{1,0:T(8,128)(2,1)} %get-tuple-element.165.refs_0_, bf16[512,768]{1,0:T(8,128)(2,1)} %bitcast.47, f32[512,768]{1,0:T(8,128)} %get-tuple-element.170.refs_2_, bf16[768,2304]{1,0:T(8,128)(2,1)} %get-tuple-element.171.refs_3_, ...), custom_call_target="tpu_custom_call" | custom-call | flops 1 | bytes 1291500 | tf_op jit(solution)/shard_map/project_back/pallas_call | solution.py:808
  219.5 2.5 collective-permute-start.37
  224.4 6.3 %collective-permute-done.32 = bf16[8,24,1536]{2,1,0:T(8,128)(2,1)S(1)} collective-permute-done((bf16[8,24,1536]{2,1,0:T(8,128)(2,1)S(1)}, bf16[8,24,1536]{2,1,0:T(8,128)(2,1)S(1)}, u32[]{:S(2)}, u32[]{:S(2)}) %collective-permute-start.32) | collective-permute-done | bytes 589856 | tf_op jit(solution)/shard_map/ppermute | solution.py:828
  234.5 4.8 %collective-permute-done.34 = bf16[4,24,1536]{2,1,0:T(8,128)(2,1)S(1)} collective-permute-done((bf16[4,24,1536]{2,1,0:T(8,128)(2,1)S(1)}, bf16[4,24,1536]{2,1,0:T(8,128)(2,1)S(1)}, u32[]{:S(2)}, u32[]{:S(2)}) %collective-permute-start.34) | collective-permute-done | bytes 294944 | tf_op jit(solution)/shard_map/ppermute | solution.py:828
  241.8 2.7 %collective-permute-start.36 = (bf16[24,3072]{1,0:T(8,128)(2,1)S(1)}, bf16[24,3072]{1,0:T(8,128)(2,1)S(1)}, u32[]{:S(2)}, u32[]{:S(2)}) collective-permute-start(bf16[24,3072]{1,0:T(8,128)(2,1)S(1)} %get-tuple-element.192), channel_id=1, source_target_pairs={{0,8},{2,10},{4,12},{6,14},{8,0},{10,2},{12,4},{14,6},{16,24},{18,... | collective-permute-start | bytes 442376 | tf_op jit(solution)/shard_map/ppermute | solution.py:828
  247.6 3.0 %collective-permute-done.36.refs_1_ = bf16[24,3072]{1,0:T(8,128)(2,1)S(1)} collective-permute-done((bf16[24,3072]{1,0:T(8,128)(2,1)S(1)}, bf16[24,3072]{1,0:T(8,128)(2,1)S(1)}, u32[]{:S(2)}, u32[]{:S(2)}) %collective-permute-start.36) | collective-permute-done | bytes 147488 | tf_op jit(solution)/shard_map/ppermute | solution.py:828
  256.5 2.7 %finish.1 = (f32[24,1536]{1,0:T(8,128)}, f32[24,768]{1,0:T(8,128)}, f32[24,768]{1,0:T(8,128)}, f32[1,24]{1,0:T(1,128)}, f32[1,24]{1,0:T(1,128)}) custom-call(s32[8]{0:T(128)} %pad_add_fusion.s_ref, bf16[24,3072]{1,0:T(8,128)(2,1)} %get-tuple-element.235.refs_0_, bf16[24,3072]{1,0:T(8,128)(2,1)} %copy-done.27, bf16[24,3072]{1,0:T(8,128)(2,1)} %copy-done.28, ...), custom_call_target="tpu_custom_call" | custom-call | flops 1 | bytes 369000 | tf_op jit(solution)/shard_map/finish/pallas_call | solution.py:778
  (221 shorter events, 79.2 us)
Async XLA Ops:
  7.2 96.5 %all-gather.2.cloned.1.call-start = ((), (), s32[]{:S(2)}) async-start(), calls=%async_computation.2 | async-start | bytes 2506752 | tf_op jit(solution)/shard_map/all_gather | solution.py:896
  9.0 11.7 %collective-permute-start.1 = (bf16[24,2560]{1,0:T(8,128)(2,1)S(1)}, bf16[24,2560]{1,0:T(8,128)(2,1)S(1)}, u32[]{:S(2)}, u32[]{:S(2)}) collective-permute-start(bf16[24,2560]{1,0:T(8,128)(2,1)S(1)} %get-tuple-element.241), channel_id=1, source_target_pairs={{0,16},{2,18},{4,20},{6,22},{8,24},{10,26},{12,28},{14,30},{16,0},... | collective-permute-start | bytes 368648 | tf_op jit(solution)/shard_map/ppermute | solution.py:828
  31.1 21.7 %collective-permute-start.6 = (bf16[8,24,1280]{2,1,0:T(8,128)(2,1)S(1)}, bf16[8,24,1280]{2,1,0:T(8,128)(2,1)S(1)}, u32[]{:S(2)}, u32[]{:S(2)}) collective-permute-start(bf16[8,24,1280]{2,1,0:T(8,128)(2,1)S(1)} %pad_maximum_fusion.9), channel_id=1, source_target_pairs={{0,4},{2,6},{4,0},{6,2},{8,12},{10,14},{12,8},{14,10},{16,20},{18,... | collective-permute-start | bytes 1474568 | tf_op jit(solution)/shard_map/ppermute | solution.py:828
  32.7 20.1 %collective-permute-start.5 = (bf16[8,24,1280]{2,1,0:T(8,128)(2,1)S(1)}, bf16[8,24,1280]{2,1,0:T(8,128)(2,1)S(1)}, u32[]{:S(2)}, u32[]{:S(2)}) collective-permute-start(bf16[8,24,1280]{2,1,0:T(8,128)(2,1)S(1)} %pad_maximum_fusion.8), channel_id=1, source_target_pairs={{0,2},{2,0},{4,6},{6,4},{8,10},{10,8},{12,14},{14,12},{16,18},{18,... | collective-permute-start | bytes 1474568 | tf_op jit(solution)/shard_map/ppermute | solution.py:828
  35.6 16.1 %collective-permute-start.8 = (bf16[48,1920]{1,0:T(8,128)(2,1)S(1)}, bf16[48,1920]{1,0:T(8,128)(2,1)S(1)}, u32[]{:S(2)}, u32[]{:S(2)}) collective-permute-start(bf16[48,1920]{1,0:T(8,128)(2,1)S(1)} %maximum_maximum_fusion), channel_id=1, source_target_pairs={{0,16},{2,18},{4,20},{6,22},{8,24},{10,26},{12,28},{14,30},{16,0},... | collective-permute-start | bytes 552968 | tf_op jit(solution)/shard_map/ppermute | solution.py:828
  38.4 13.3 %collective-permute-start.7 = (bf16[48,1920]{1,0:T(8,128)(2,1)S(1)}, bf16[48,1920]{1,0:T(8,128)(2,1)}, u32[]{:S(2)}, u32[]{:S(2)}) collective-permute-start(bf16[48,1920]{1,0:T(8,128)(2,1)S(1)} %maximum_maximum_fusion), channel_id=1, source_target_pairs={{0,8},{2,10},{4,12},{6,14},{8,0},{10,2},{12,4},{14,6},{16,24},{18,... | collective-permute-start | bytes 552968 | tf_op jit(solution)/shard_map/ppermute | solution.py:828
  39.0 138.7 %reduce-scatter.3.cloned.1.call-start = ((), (), s32[]{:S(2)}) async-start(), calls=%async_computation.3 | async-start | bytes 2949120 | tf_op jit(solution)/shard_map/reduce_scatter | solution.py:957
  53.9 11.6 %collective-permute-start.12 = (bf16[4,48,1024]{2,1,0:T(8,128)(2,1)S(1)}, bf16[4,48,1024]{2,1,0:T(8,128)(2,1)S(1)}, u32[]{:S(2)}, u32[]{:S(2)}) collective-permute-start(bf16[4,48,1024]{2,1,0:T(8,128)(2,1)S(1)} %slice.185.refs_0_), channel_id=1, source_target_pairs={{0,2},{2,0},{4,6},{6,4},{8,10},{10,8},{12,14},{14,12},{16,18},{18,... | collective-permute-start | bytes 1179656 | tf_op jit(solution)/shard_map/ppermute | solution.py:828
  68.7 23.5 %collective-permute-start.15 = (bf16[8,48,1024]{2,1,0:T(8,128)(2,1)}, bf16[8,48,1024]{2,1,0:T(8,128)(2,1)}, u32[]{:S(2)}, u32[]{:S(2)}) collective-permute-start(bf16[8,48,1024]{2,1,0:T(8,128)(2,1)} %pad_maximum_fusion.2), channel_id=1, source_target_pairs={{0,4},{2,6},{4,0},{6,2},{8,12},{10,14},{12,8},{14,10},{16,20},{18,... | collective-permute-start | bytes 2359304 | tf_op jit(solution)/shard_map/ppermute | solution.py:828
  70.3 20.4 %collective-permute-start.16 = (bf16[8,48,896]{2,1,0:T(8,128)(2,1)}, bf16[8,48,896]{2,1,0:T(8,128)(2,1)S(1)}, u32[]{:S(2)}, u32[]{:S(2)}) collective-permute-start(bf16[8,48,896]{2,1,0:T(8,128)(2,1)} %pad_maximum_fusion.4), channel_id=1, source_target_pairs={{0,2},{2,0},{4,6},{6,4},{8,10},{10,8},{12,14},{14,12},{16,18},{18,... | collective-permute-start | bytes 2064392 | tf_op jit(solution)/shard_map/ppermute | solution.py:828
  100.6 15.1 %collective-permute-start.20 = (bf16[512,768]{1,0:T(8,128)(2,1)S(1)}, bf16[512,768]{1,0:T(8,128)(2,1)S(1)}, u32[]{:S(2)}, u32[]{:S(2)}) collective-permute-start(bf16[512,768]{1,0:T(8,128)(2,1)S(1)} %bitcast_select_fusion.n_ref.ng_ref.c_ref), channel_id=1, source_target_pairs={{0,1},{1,0},{2,3},{3,2},{4,5},{5,4},{6,7},{7,6},{8,9},{9,8},{10,11... | collective-permute-start | bytes 2359304 | tf_op jit(solution)/shard_map/ppermute | solution.py:824
  131.1 103.3 %reduce-scatter.5.cloned.1.call-start = ((), (), s32[]{:S(2)}) async-start(), calls=%async_computation.4 | async-start | bytes 737280 | tf_op jit(solution)/shard_map/reduce_scatter | solution.py:984
  132.2 23.6 %collective-permute-start.21 = (bf16[512,768]{1,0:T(8,128)(2,1)S(1)}, bf16[512,768]{1,0:T(8,128)(2,1)S(1)}, u32[]{:S(2)}, u32[]{:S(2)}) collective-permute-start(bf16[512,768]{1,0:T(8,128)(2,1)S(1)} %copy-done.37), channel_id=1, source_target_pairs={{0,1},{1,0},{2,3},{3,2},{4,5},{5,4},{6,7},{7,6},{8,9},{9,8},{10,11... | collective-permute-start | bytes 2359304 | tf_op jit(solution)/shard_map/ppermute | solution.py:824
  154.1 23.5 %collective-permute-start.24 = (bf16[400,768]{1,0:T(8,128)(2,1)}, bf16[400,768]{1,0:T(8,128)(2,1)S(1)}, u32[]{:S(2)}, u32[]{:S(2)}) collective-permute-start(bf16[400,768]{1,0:T(8,128)(2,1)} %get-tuple-element.153), channel_id=1, source_target_pairs={{0,2},{2,0},{4,6},{6,4},{8,10},{10,8},{12,14},{14,12},{16,18},{18,... | collective-permute-start | bytes 1843208 | tf_op jit(solution)/shard_map/ppermute | solution.py:828
  155.3 22.4 %collective-permute-start.25 = (bf16[400,768]{1,0:T(8,128)(2,1)}, bf16[400,768]{1,0:T(8,128)(2,1)S(1)}, u32[]{:S(2)}, u32[]{:S(2)}) collective-permute-start(bf16[400,768]{1,0:T(8,128)(2,1)} %get-tuple-element.154), channel_id=1, source_target_pairs={{0,4},{2,6},{4,0},{6,2},{8,12},{10,14},{12,8},{14,10},{16,20},{18,... | collective-permute-start | bytes 1843208 | tf_op jit(solution)/shard_map/ppermute | solution.py:828
  178.5 11.5 %collective-permute-start.26 = (bf16[512,1536]{1,0:T(8,128)(2,1)}, bf16[512,1536]{1,0:T(8,128)(2,1)S(1)}, u32[]{:S(2)}, u32[]{:S(2)}) collective-permute-start(bf16[512,1536]{1,0:T(8,128)(2,1)} %get-tuple-element.157), channel_id=1, source_target_pairs={{1,0},{3,2},{5,4},{7,6},{9,8},{11,10},{13,12},{15,14},{17,16},{19,... | collective-permute-start | bytes 4718600 | tf_op jit(solution)/shard_map/ppermute | solution.py:983
  201.6 10.9 %collective-permute-start.29 = (bf16[8,24,3072]{2,1,0:T(8,128)(2,1)}, bf16[8,24,3072]{2,1,0:T(8,128)(2,1)S(1)}, u32[]{:S(2)}, u32[]{:S(2)}) collective-permute-start(bf16[8,24,3072]{2,1,0:T(8,128)(2,1)} %get-tuple-element.174), channel_id=1, source_target_pairs={{0,1},{1,0},{2,3},{3,2},{4,5},{5,4},{6,7},{7,6},{8,9},{9,8},{10,11... | collective-permute-start | bytes 3538952 | tf_op jit(solution)/shard_map/ppermute | solution.py:824
  201.8 10.8 %collective-permute-start.27 = (bf16[8,24,1536]{2,1,0:T(8,128)(2,1)}, bf16[8,24,1536]{2,1,0:T(8,128)(2,1)S(1)}, u32[]{:S(2)}, u32[]{:S(2)}) collective-permute-start(bf16[8,24,1536]{2,1,0:T(8,128)(2,1)} %get-tuple-element.172), channel_id=1, source_target_pairs={{0,1},{1,0},{2,3},{3,2},{4,5},{5,4},{6,7},{7,6},{8,9},{9,8},{10,11... | collective-permute-start | bytes 1769480 | tf_op jit(solution)/shard_map/ppermute | solution.py:824
  216.1 14.6 %collective-permute-start.32 = (bf16[8,24,1536]{2,1,0:T(8,128)(2,1)S(1)}, bf16[8,24,1536]{2,1,0:T(8,128)(2,1)S(1)}, u32[]{:S(2)}, u32[]{:S(2)}) collective-permute-start(bf16[8,24,1536]{2,1,0:T(8,128)(2,1)S(1)} %add_convert_fusion.4), channel_id=1, source_target_pairs={{0,2},{2,0},{4,6},{6,4},{8,10},{10,8},{12,14},{14,12},{16,18},{18,... | collective-permute-start | bytes 1769480 | tf_op jit(solution)/shard_map/ppermute | solution.py:828
  217.1 14.5 %collective-permute-start.33 = (bf16[8,24,1536]{2,1,0:T(8,128)(2,1)S(1)}, bf16[8,24,1536]{2,1,0:T(8,128)(2,1)S(1)}, u32[]{:S(2)}, u32[]{:S(2)}) collective-permute-start(bf16[8,24,1536]{2,1,0:T(8,128)(2,1)S(1)} %add_convert_fusion.3), channel_id=1, source_target_pairs={{0,4},{2,6},{4,0},{6,2},{8,12},{10,14},{12,8},{14,10},{16,20},{18,... | collective-permute-start | bytes 1769480 | tf_op jit(solution)/shard_map/ppermute | solution.py:828
  219.5 26.5 %collective-permute-start.37 = (bf16[64,1536]{1,0:T(8,128)(2,1)}, bf16[64,1536]{1,0:T(8,128)(2,1)S(1)}, u32[]{:S(2)}, u32[]{:S(2)}) collective-permute-start(bf16[64,1536]{1,0:T(8,128)(2,1)} %get-tuple-element.196), channel_id=1, source_target_pairs={{0,8},{2,10},{4,12},{6,14},{8,0},{10,2},{12,4},{14,6},{16,24},{18,... | collective-permute-start | bytes 589832 | tf_op jit(solution)/shard_map/ppermute | solution.py:828
  222.0 25.6 %collective-permute-start.38 = (bf16[64,1536]{1,0:T(8,128)(2,1)}, bf16[64,1536]{1,0:T(8,128)(2,1)}, u32[]{:S(2)}, u32[]{:S(2)}) collective-permute-start(bf16[64,1536]{1,0:T(8,128)(2,1)} %get-tuple-element.197), channel_id=1, source_target_pairs={{0,16},{2,18},{4,20},{6,22},{8,24},{10,26},{12,28},{14,30},{16,0},... | collective-permute-start | bytes 589832 | tf_op jit(solution)/shard_map/ppermute | solution.py:828
  222.3 25.3 %collective-permute-start.39 = (bf16[64,1536]{1,0:T(8,128)(2,1)}, bf16[64,1536]{1,0:T(8,128)(2,1)}, u32[]{:S(2)}, u32[]{:S(2)}) collective-permute-start(bf16[64,1536]{1,0:T(8,128)(2,1)} %get-tuple-element.198), channel_id=1, source_target_pairs={{0,24},{2,26},{4,28},{6,30},{8,16},{10,18},{12,20},{14,22},{16,8},... | collective-permute-start | bytes 589832 | tf_op jit(solution)/shard_map/ppermute | solution.py:828
  244.5 11.2 %collective-permute-start.40 = (bf16[24,3072]{1,0:T(8,128)(2,1)S(1)}, bf16[24,3072]{1,0:T(8,128)(2,1)S(1)}, u32[]{:S(2)}, u32[]{:S(2)}) collective-permute-start(bf16[24,3072]{1,0:T(8,128)(2,1)S(1)} %get-tuple-element.200), channel_id=1, source_target_pairs={{0,16},{2,18},{4,20},{6,22},{8,24},{10,26},{12,28},{14,30},{16,0},... | collective-permute-start | bytes 442376 | tf_op jit(solution)/shard_map/ppermute | solution.py:828
  (64 other events, 391.4 us)
Sparse Core Ops, SparseCore 0:
  39.1 64.5 all-gather.1
  131.2 43.9 reduce-scatter.2
  204.4 22.5 reduce-scatter.4

commit v2 on v1

--- a/solution.py
+++ b/solution.py
@@ -13,6 +13,7 @@
 F32 = jnp.float32
 BF16 = jnp.bfloat16
 VMEM_LIMIT = 60 * 1024 * 1024
+VMEM_LIMITS = {"project_grads": 30 * 1024 * 1024, "finish": 30 * 1024 * 1024}
 TILE = 256
 EXTRA = 16
 COST_SCALE = 0.05
@@ -56,7 +57,7 @@
             scratch_shapes=list(scratch),
         ),
         input_output_aliases=aliases or {},
-        compiler_params=pltpu.CompilerParams(vmem_limit_bytes=VMEM_LIMIT),
+        compiler_params=pltpu.CompilerParams(vmem_limit_bytes=VMEM_LIMITS.get(name, VMEM_LIMIT)),
         cost_estimate=pl.CostEstimate(
             flops=1, bytes_accessed=int(COST_SCALE * COSTS[name] * 3690000), transcendentals=0
         ),
@@ -190,21 +191,26 @@
                 allowed = (key_at <= place) & (key_at + offset < length)
                 sums = []
                 logs = []
+                near_scores, far_scores = [], []
                 for head in range(2):
                     mine = jnp.where(
                         lane_of(head), query[t * tile : end], jnp.zeros((), BF16)
                     )
-                    scores = jnp.where(allowed, mm_tail(mine, kv_ref[0:end, 0:PAIR]), MASKED)
+                    near_scores.append(mm_tail(mine, kv_ref[0:end, 0:PAIR]))
+                    if far:
+                        far_scores.append(mm_tail(mine, fkv_ref[:, 0:PAIR]))
+                for head in range(2):
+                    scores = jnp.where(allowed, near_scores[head], MASKED)
                     highest = jnp.max(scores, -1, keepdims=True)
                     if far:
-                        beyond = mm_tail(mine, fkv_ref[:, 0:PAIR])
+                        beyond = far_scores[head]
                         highest = jnp.maximum(highest, jnp.max(beyond, -1, keepdims=True))
                         beyond = jnp.exp(beyond - highest)
                     scores = jnp.exp(scores - highest)
-                    total = jnp.sum(scores, -1, keepdims=True)
+                    total = jnp.sum(fold(scores), -1, keepdims=True)
                     mixed = mm(scores.astype(BF16), kv_ref[0:end, PAIR : 2 * PAIR])
                     if far:
-                        total = total + jnp.sum(beyond, -1, keepdims=True)
+                        total = total + jnp.sum(fold(beyond), -1, keepdims=True)
                         mixed = mixed + mm(beyond.astype(BF16), fkv_ref[:, PAIR : 2 * PAIR])
                     sums.append(mixed / total)
                     logs.append(jnp.broadcast_to(highest + jnp.log(total), (tile, PAIR)))
@@ -282,17 +288,20 @@
                     key_at = lax.broadcasted_iota(jnp.int32, (tile, count), 0) + at
                     place = lax.broadcasted_iota(jnp.int32, (tile, count), 1) + low
                     allowed = (key_at <= place) & (key_at + offset < length)
+                all_scores, all_grads = [], []
                 for head in range(2):
                     lanes = lane_of(head)
                     mine = jnp.where(lanes, query[low:rows], jnp.zeros((), BF16))
                     mine_grad = jnp.where(lanes, grad[low:rows], jnp.zeros((), BF16))
-                    scores = mm_tail(key, mine)
+                    all_scores.append(mm_tail(key, mine))
+                    all_grads.append(mm_tail(value, mine_grad))
+                for head in range(2):
+                    scores = all_scores[head]
                     if masked:
                         scores = jnp.where(allowed, scores, MASKED)
                     base = head * HEAD_DIM
                     probs = jnp.exp(scores - l_ref[0, 4 * head : 4 * head + 1, low:rows])
-                    prob_grad = mm_tail(value, mine_grad)
-                    score_grad = (probs * (prob_grad - dots[head : head + 1, low:rows])).astype(BF16)
+                    score_grad = (probs * (all_grads[head] - dots[head : head + 1, low:rows])).astype(BF16)
                     vgrads.append(mm(probs.astype(BF16), grad[low:rows]))
                     kgrads.append(mm(score_grad, query[low:rows]))
                     part = mm(key_turned[base : base + HEAD_DIM], score_grad)
@@ -1001,7 +1010,7 @@
             (inputs_grad, other_one, other_two, other, got[0], got[1])
         )
         upper_one, upper_two = add_low(keep_one, other_one), add_low(keep_two, other_two)
-        upper_one, upper_two = barrier((upper_one, upper_two))
+        upper_one, upper_two, keep, other = barrier((upper_one, upper_two, keep, other))
         got_one, got_two = exchange(upper_one, 1, chips), exchange(upper_two, 2, chips)
         in_held, fourth = add_parts(in_kept, fourth, got, 0, count // 2)
         in_held = in_held.reshape(chips // 4, depth, units)

time: 267 us -> 263 us (0.985)
  Pallas kernels: 110 us -> 99.9 us
  other arithmetic: 17.8 us -> 21.9 us
    pallas_call x1, Pallas kernels: 10.5 us -> 5.6 us  [project_grads(): call(body, 'project_grads', (shaped((rows, 3 * cols), BF16),) + tuple((sh...]
    pallas_call x1, Pallas kernels: 11.6 us -> 8.66 us  [attend(): call(body, 'attend', (shaped((rows, width), BF16), shaped((pairs, 8, rows...]
    ppermute x1, waiting for transfers between devices: 7.45 us -> 4.51 us  [on_device(): far_dkv = lax.ppermute(far_dkv, CORES, [(1, 0)])]
    unnamed x76 -> x82, local copies, waits for them, and re-layouts: 9.45 us -> 9.88 us
  transfers between devices with their start and end apart: 46 -> 46, of which waited for: 24 -> 25; matrix products, arithmetic and copies ran while one was open for 6% -> 9% of each run, Pallas kernels for 31% -> 30%
where the time goes in v2:
time: 263 us; the launch traced here: 262 us
  Pallas kernels  99.9 us (38%)
  waiting for transfers between devices  63.5 us (24%)
  starting transfers between devices  46.7 us (18%)
  other arithmetic  21.9 us (8%)
  local copies, waits for them, and re-layouts  15.1 us (6%)
  between operations  15 us (6%)
    ppermute x28, waiting for transfers between devices, exchange(): return lax.ppermute(array, CHIPS, [(i, i ^ mask) for i in range(chips)])  51.9 us
    ppermute x28, starting transfers between devices, exchange(): return lax.ppermute(array, CHIPS, [(i, i ^ mask) for i in range(chips)])  38.1 us
    pallas_call x1, Pallas kernels, ffn_back(): call(body, 'ffn_back', (shaped((rows, width), BF16), shaped((rows, width)...  20.3 us
    pallas_call x1, Pallas kernels, ffn_out(): call(body, 'ffn_out', (shaped((rows, width), BF16), shaped((rows, width),...  14 us
    pallas_call x1, Pallas kernels, attend_back(): call(body, 'attend_back', (shaped((rows, width), BF16), shaped((rows, 2 *...  11.9 us
    pallas_call x1, Pallas kernels, ffn_in(): call(body, 'ffn_in', (shaped((2 * rows, units), BF16), shaped((2 * rows,...  10.4 us
    unnamed x82, local copies, waits for them, and re-layouts  9.88 us
    pallas_call x1, Pallas kernels, attend(): call(body, 'attend', (shaped((rows, width), BF16), shaped((pairs, 8, rows...  8.66 us
  transfers between devices with their start and end apart: 46, of which 25 were waited for; matrix products, arithmetic and copies ran while one was open for 9% of the time, Pallas kernels for 30%

profile of v2, /device:TPU:0, one launch (start us, length us, event | category | flops | bytes accessed | tf_op | source)
XLA Modules:
  0.0 262.1 jit_solution(12358057639311791327)
XLA Ops:
  9.0 4.1 %collective-permute-start.1 = (bf16[24,2560]{1,0:T(8,128)(2,1)S(1)}, bf16[24,2560]{1,0:T(8,128)(2,1)S(1)}, u32[]{:S(2)}, u32[]{:S(2)}) collective-permute-start(bf16[24,2560]{1,0:T(8,128)(2,1)S(1)} %get-tuple-element.245), channel_id=1, source_target_pairs={{0,16},{2,18},{4,20},{6,22},{8,24},{10,26},{12,28},{14,30},{16,0},... | collective-permute-start | bytes 368648 | tf_op jit(solution)/shard_map/ppermute | solution.py:837
  16.3 4.4 %collective-permute-done.1 = bf16[24,2560]{1,0:T(8,128)(2,1)S(1)} collective-permute-done((bf16[24,2560]{1,0:T(8,128)(2,1)S(1)}, bf16[24,2560]{1,0:T(8,128)(2,1)S(1)}, u32[]{:S(2)}, u32[]{:S(2)}) %collective-permute-start.1) | collective-permute-done | bytes 122912 | tf_op jit(solution)/shard_map/ppermute | solution.py:837
  26.0 3.8 %collective-permute-done.4 = bf16[4,24,1280]{2,1,0:T(8,128)(2,1)S(1)} collective-permute-done((bf16[4,24,1280]{2,1,0:T(8,128)(2,1)S(1)}, bf16[4,24,1280]{2,1,0:T(8,128)(2,1)S(1)}, u32[]{:S(2)}, u32[]{:S(2)}) %collective-permute-start.4) | collective-permute-done | bytes 245792 | tf_op jit(solution)/shard_map/ppermute | solution.py:837
  33.2 2.4 collective-permute-start.9
  35.6 2.8 %collective-permute-start.8 = (bf16[48,1920]{1,0:T(8,128)(2,1)S(1)}, bf16[48,1920]{1,0:T(8,128)(2,1)S(1)}, u32[]{:S(2)}, u32[]{:S(2)}) collective-permute-start(bf16[48,1920]{1,0:T(8,128)(2,1)S(1)} %maximum_maximum_fusion), channel_id=1, source_target_pairs={{0,16},{2,18},{4,20},{6,22},{8,24},{10,26},{12,28},{14,30},{16,0},... | collective-permute-start | bytes 552968 | tf_op jit(solution)/shard_map/ppermute | solution.py:837
  41.3 10.5 %collective-permute-done.8 = bf16[48,1920]{1,0:T(8,128)(2,1)S(1)} collective-permute-done((bf16[48,1920]{1,0:T(8,128)(2,1)S(1)}, bf16[48,1920]{1,0:T(8,128)(2,1)S(1)}, u32[]{:S(2)}, u32[]{:S(2)}) %collective-permute-start.8) | collective-permute-done | bytes 184352 | tf_op jit(solution)/shard_map/ppermute | solution.py:837
  57.2 8.2 %project.1 = (bf16[512,768]{1,0:T(8,128)(2,1)}, bf16[512,1536]{1,0:T(8,128)(2,1)}, bf16[512,768]{1,0:T(8,128)(2,1)}, bf16[768,2304]{1,0:T(8,128)(2,1)}, f32[8,768]{1,0:T(8,128)}) custom-call(s32[8]{0:T(128)} %pad_add_fusion.s_ref, bf16[512,768]{1,0:T(8,128)(2,1)} %bitcast.45, bf16[16,24,1280]{2,1,0:T(8,128)(2,1)} %copy-done.14, ...), custom_call_target="tpu_custom_call" | custom-call | flops 1 | bytes 1476000 | tf_op jit(solution)/shard_map/project/pallas_call | solution.py:154
  72.5 8.7 %attend.1 = (bf16[512,768]{1,0:T(8,128)(2,1)}, f32[6,8,512]{2,1,0:T(8,128)}) custom-call(s32[8]{0:T(128)} %pad_add_fusion.s_ref, bf16[512,768]{1,0:T(8,128)(2,1)} %get-tuple-element.123.q_ref, bf16[512,1536]{1,0:T(8,128)(2,1)} %get-tuple-element.125.kv_ref, bf16[512,1536]{1,0:T(8,128)(2,1)} %copy-done.12), custom_call_target="tpu_custom_call" | custom-call | flops 1 | bytes 2767500 | tf_op jit(solution)/shard_map/attend/pallas_call | solution.py:233
  81.1 9.7 %collective-permute-done.16.refs_5_ = bf16[8,48,896]{2,1,0:T(8,128)(2,1)S(1)} collective-permute-done((bf16[8,48,896]{2,1,0:T(8,128)(2,1)}, bf16[8,48,896]{2,1,0:T(8,128)(2,1)S(1)}, u32[]{:S(2)}, u32[]{:S(2)}) %collective-permute-start.16) | collective-permute-done | bytes 688160 | tf_op jit(solution)/shard_map/ppermute | solution.py:837
  95.2 5.1 %join.1 = (bf16[512,768]{1,0:T(8,128)(2,1)}, f32[512,768]{1,0:T(8,128)}, bf16[512,768]{1,0:T(8,128)(2,1)}, bf16[768,768]{1,0:T(8,128)(2,1)}) custom-call(s32[8]{0:T(128)} %pad_add_fusion.s_ref, bf16[512,768]{1,0:T(8,128)(2,1)} %get-tuple-element.131.a_ref.o_ref, bf16[512,768]{1,0:T(8,128)(2,1)} %bitcast.46, f32[8,768]{1,0:T(8,128)} %get-tuple-element.132.g_ref.refs_4_, ...), custom_call_target="tpu_custom_call" | custom-call | flops 1 | bytes 922500 | tf_op jit(solution)/shard_map/join/pallas_call | solution.py:364
  101.1 2.6 %all-gather.2.cloned.1.call-done = bf16[768,1536]{1,0:T(8,128)(2,1)} async-done(((bf16[48,1536]{1,0:T(8,128)(2,1)}), bf16[768,1536]{1,0:T(8,128)(2,1)}) %all-gather.2.cloned.1.call-update) | async-done | bytes 2359312 | tf_op jit(solution)/shard_map/all_gather | solution.py:905
  104.7 10.4 %ffn_in.1 = (bf16[1024,1536]{1,0:T(8,128)(2,1)}, bf16[1024,1536]{1,0:T(8,128)(2,1)}, f32[8,1024]{1,0:T(8,128)}, bf16[768,1536]{1,0:T(8,128)(2,1)}) custom-call(s32[8]{0:T(128)} %pad_add_fusion.s_ref, bf16[512,768]{1,0:T(8,128)(2,1)} %get-tuple-element.134.n_ref, bf16[512,768]{1,0:T(8,128)(2,1)} %copy-done.17, bf16[4,48,1024]{2,1,0:T(8,128)(2,1)} %copy-done.16, ...), custom_call_target="tpu_custom_call" | custom-call | flops 1 | bytes 1845000 | tf_op jit(solution)/shard_map/ffn_in/pallas_call | solution.py:505
  117.2 14.0 %ffn_out.1 = (bf16[512,768]{1,0:T(8,128)(2,1)}, bf16[512,768]{1,0:T(8,128)(2,1)}, f32[8,1024]{1,0:T(8,128)}, bf16[768,1536]{1,0:T(8,128)(2,1)}) custom-call(s32[8]{0:T(128)} %pad_add_fusion.s_ref, bf16[1024,1536]{1,0:T(8,128)(2,1)} %get-tuple-element.137.a_ref, f32[8,1024]{1,0:T(8,128)} %get-tuple-element.138.st_ref, f32[8,1024]{1,0:T(8,128)} %copy-done.33, ...), custom_call_target="tpu_custom_call" | custom-call | flops 1 | bytes 1845000 | tf_op jit(solution)/shard_map/ffn_out/pallas_call | solution.py:560
  133.7 20.3 %ffn_back.1 = (bf16[512,768]{1,0:T(8,128)(2,1)}, bf16[512,768]{1,0:T(8,128)(2,1)}, f32[8,1536]{1,0:T(8,128)}, bf16[384,1536]{1,0:T(8,128)(2,1)}, bf16[400,768]{1,0:T(8,128)(2,1)}, /*index=5*/bf16[400,768]{1,0:T(8,128)(2,1)}) custom-call(s32[8]{0:T(128)} %pad_add_fusion.s_ref, bf16[1024,1536]{1,0:T(8,128)(2,1)} %get-tuple-element.137.a_ref, ...), custom_call_target="tpu_custom_call" | custom-call | flops 1 | bytes 2583000 | tf_op jit(solution)/shard_map/ffn_back/pallas_call | solution.py:659
  157.5 7.3 %join_back.1 = (bf16[512,768]{1,0:T(8,128)(2,1)}, f32[512,768]{1,0:T(8,128)}, bf16[512,768]{1,0:T(8,128)(2,1)}, bf16[512,768]{1,0:T(8,128)(2,1)}) custom-call(s32[8]{0:T(128)} %pad_add_fusion.s_ref, bf16[512,768]{1,0:T(8,128)(2,1)} %get-tuple-element.140.b_ref, bf16[512,768]{1,0:T(8,128)(2,1)} %copy-done.25, bf16[512,768]{1,0:T(8,128)(2,1)} %get-tuple-element.145.f_ref, ...), custom_call_target="tpu_custom_call" | custom-call | flops 1 | bytes 1291500 | tf_op jit(solution)/shard_map/join_back/pallas_call | solution.py:405
  164.9 11.9 %attend_back.1 = (bf16[512,768]{1,0:T(8,128)(2,1)}, bf16[512,1536]{1,0:T(8,128)(2,1)}, bf16[512,1536]{1,0:T(8,128)(2,1)}) custom-call(s32[8]{0:T(128)} %pad_add_fusion.s_ref, bf16[512,768]{1,0:T(8,128)(2,1)} %get-tuple-element.123.q_ref, bf16[512,1536]{1,0:T(8,128)(2,1)} %get-tuple-element.125.kv_ref, bf16[512,1536]{1,0:T(8,128)(2,1)} %copy-done.12, ...), custom_call_target="tpu_custom_call" | custom-call | flops 1 | bytes 3690000 | tf_op jit(solution)/shard_map/attend_back/pallas_call | solution.py:330
  184.8 4.5 %collective-permute-done.26.fkv_ref = bf16[512,1536]{1,0:T(8,128)(2,1)S(1)} collective-permute-done((bf16[512,1536]{1,0:T(8,128)(2,1)}, bf16[512,1536]{1,0:T(8,128)(2,1)S(1)}, u32[]{:S(2)}, u32[]{:S(2)}) %collective-permute-start.26) | collective-permute-done | bytes 1572896 | tf_op jit(solution)/shard_map/ppermute | solution.py:992
  189.3 5.6 %project_grads.1 = (bf16[512,2304]{1,0:T(8,128)(2,1)S(1)}, bf16[8,24,3072]{2,1,0:T(8,128)(2,1)S(1)}, bf16[8,24,1536]{2,1,0:T(8,128)(2,1)S(1)}, bf16[8,24,1536]{2...) custom-call(s32[8]{0:T(128)S(1)} %copy-done.9, ...), custom_call_target="tpu_custom_call" | custom-call | flops 1 | bytes 2029500 | tf_op jit(solution)/shard_map/project_grads/pallas_call | solution.py:744
  201.0 7.1 %project_back.1 = bf16[512,768]{1,0:T(8,128)(2,1)} custom-call(s32[8]{0:T(128)} %pad_add_fusion.s_ref, bf16[512,2304]{1,0:T(8,128)(2,1)} %copy-done, bf16[512,768]{1,0:T(8,128)(2,1)} %bitcast.47, f32[512,768]{1,0:T(8,128)} %get-tuple-element.172.refs_2_, bf16[768,2304]{1,0:T(8,128)(2,1)} %get-tuple-element.173.refs_3_, f32[8,768]{1,0:T(8,128)} %get-tuple-element.132.g_ref.refs_4_), custom_call_target="tpu_custom_call" | custom-call | flops 1 | bytes 1291500 | tf_op jit(solution)/shard_map/project_back/pallas_call | solution.py:817
  219.4 2.6 collective-permute-start.37
  224.4 5.2 %collective-permute-done.32 = bf16[8,24,1536]{2,1,0:T(8,128)(2,1)S(1)} collective-permute-done((bf16[8,24,1536]{2,1,0:T(8,128)(2,1)S(1)}, bf16[8,24,1536]{2,1,0:T(8,128)(2,1)S(1)}, u32[]{:S(2)}, u32[]{:S(2)}) %collective-permute-start.32) | collective-permute-done | bytes 589856 | tf_op jit(solution)/shard_map/ppermute | solution.py:837
  235.5 3.2 %collective-permute-done.34 = bf16[4,24,1536]{2,1,0:T(8,128)(2,1)S(1)} collective-permute-done((bf16[4,24,1536]{2,1,0:T(8,128)(2,1)S(1)}, bf16[4,24,1536]{2,1,0:T(8,128)(2,1)S(1)}, u32[]{:S(2)}, u32[]{:S(2)}) %collective-permute-start.34) | collective-permute-done | bytes 294944 | tf_op jit(solution)/shard_map/ppermute | solution.py:837
  240.1 2.6 %collective-permute-start.36 = (bf16[24,3072]{1,0:T(8,128)(2,1)S(1)}, bf16[24,3072]{1,0:T(8,128)(2,1)S(1)}, u32[]{:S(2)}, u32[]{:S(2)}) collective-permute-start(bf16[24,3072]{1,0:T(8,128)(2,1)S(1)} %get-tuple-element.196), channel_id=1, source_target_pairs={{0,8},{2,10},{4,12},{6,14},{8,0},{10,2},{12,4},{14,6},{16,24},{18,... | collective-permute-start | bytes 442376 | tf_op jit(solution)/shard_map/ppermute | solution.py:837
  245.9 3.0 %collective-permute-done.36.refs_1_ = bf16[24,3072]{1,0:T(8,128)(2,1)S(1)} collective-permute-done((bf16[24,3072]{1,0:T(8,128)(2,1)S(1)}, bf16[24,3072]{1,0:T(8,128)(2,1)S(1)}, u32[]{:S(2)}, u32[]{:S(2)}) %collective-permute-start.36) | collective-permute-done | bytes 147488 | tf_op jit(solution)/shard_map/ppermute | solution.py:837
  (223 shorter events, 87.1 us)
Async XLA Ops:
  7.2 96.5 %all-gather.2.cloned.1.call-start = ((), (), s32[]{:S(2)}) async-start(), calls=%async_computation.2 | async-start | bytes 2506752 | tf_op jit(solution)/shard_map/all_gather | solution.py:905
  9.0 11.7 %collective-permute-start.1 = (bf16[24,2560]{1,0:T(8,128)(2,1)S(1)}, bf16[24,2560]{1,0:T(8,128)(2,1)S(1)}, u32[]{:S(2)}, u32[]{:S(2)}) collective-permute-start(bf16[24,2560]{1,0:T(8,128)(2,1)S(1)} %get-tuple-element.245), channel_id=1, source_target_pairs={{0,16},{2,18},{4,20},{6,22},{8,24},{10,26},{12,28},{14,30},{16,0},... | collective-permute-start | bytes 368648 | tf_op jit(solution)/shard_map/ppermute | solution.py:837
  31.1 21.7 %collective-permute-start.6 = (bf16[8,24,1280]{2,1,0:T(8,128)(2,1)S(1)}, bf16[8,24,1280]{2,1,0:T(8,128)(2,1)S(1)}, u32[]{:S(2)}, u32[]{:S(2)}) collective-permute-start(bf16[8,24,1280]{2,1,0:T(8,128)(2,1)S(1)} %pad_maximum_fusion.9), channel_id=1, source_target_pairs={{0,4},{2,6},{4,0},{6,2},{8,12},{10,14},{12,8},{14,10},{16,20},{18,... | collective-permute-start | bytes 1474568 | tf_op jit(solution)/shard_map/ppermute | solution.py:837
  32.7 20.1 %collective-permute-start.5 = (bf16[8,24,1280]{2,1,0:T(8,128)(2,1)S(1)}, bf16[8,24,1280]{2,1,0:T(8,128)(2,1)S(1)}, u32[]{:S(2)}, u32[]{:S(2)}) collective-permute-start(bf16[8,24,1280]{2,1,0:T(8,128)(2,1)S(1)} %pad_maximum_fusion.8), channel_id=1, source_target_pairs={{0,2},{2,0},{4,6},{6,4},{8,10},{10,8},{12,14},{14,12},{16,18},{18,... | collective-permute-start | bytes 1474568 | tf_op jit(solution)/shard_map/ppermute | solution.py:837
  35.6 16.1 %collective-permute-start.8 = (bf16[48,1920]{1,0:T(8,128)(2,1)S(1)}, bf16[48,1920]{1,0:T(8,128)(2,1)S(1)}, u32[]{:S(2)}, u32[]{:S(2)}) collective-permute-start(bf16[48,1920]{1,0:T(8,128)(2,1)S(1)} %maximum_maximum_fusion), channel_id=1, source_target_pairs={{0,16},{2,18},{4,20},{6,22},{8,24},{10,26},{12,28},{14,30},{16,0},... | collective-permute-start | bytes 552968 | tf_op jit(solution)/shard_map/ppermute | solution.py:837
  38.4 13.3 %collective-permute-start.7 = (bf16[48,1920]{1,0:T(8,128)(2,1)S(1)}, bf16[48,1920]{1,0:T(8,128)(2,1)}, u32[]{:S(2)}, u32[]{:S(2)}) collective-permute-start(bf16[48,1920]{1,0:T(8,128)(2,1)S(1)} %maximum_maximum_fusion), channel_id=1, source_target_pairs={{0,8},{2,10},{4,12},{6,14},{8,0},{10,2},{12,4},{14,6},{16,24},{18,... | collective-permute-start | bytes 552968 | tf_op jit(solution)/shard_map/ppermute | solution.py:837
  39.0 138.8 %reduce-scatter.3.cloned.1.call-start = ((), (), s32[]{:S(2)}) async-start(), calls=%async_computation.3 | async-start | bytes 2949120 | tf_op jit(solution)/shard_map/reduce_scatter | solution.py:966
  53.9 11.6 %collective-permute-start.12 = (bf16[4,48,1024]{2,1,0:T(8,128)(2,1)S(1)}, bf16[4,48,1024]{2,1,0:T(8,128)(2,1)S(1)}, u32[]{:S(2)}, u32[]{:S(2)}) collective-permute-start(bf16[4,48,1024]{2,1,0:T(8,128)(2,1)S(1)} %slice.185.refs_0_), channel_id=1, source_target_pairs={{0,2},{2,0},{4,6},{6,4},{8,10},{10,8},{12,14},{14,12},{16,18},{18,... | collective-permute-start | bytes 1179656 | tf_op jit(solution)/shard_map/ppermute | solution.py:837
  68.7 23.5 %collective-permute-start.15 = (bf16[8,48,1024]{2,1,0:T(8,128)(2,1)}, bf16[8,48,1024]{2,1,0:T(8,128)(2,1)}, u32[]{:S(2)}, u32[]{:S(2)}) collective-permute-start(bf16[8,48,1024]{2,1,0:T(8,128)(2,1)} %pad_maximum_fusion.2), channel_id=1, source_target_pairs={{0,4},{2,6},{4,0},{6,2},{8,12},{10,14},{12,8},{14,10},{16,20},{18,... | collective-permute-start | bytes 2359304 | tf_op jit(solution)/shard_map/ppermute | solution.py:837
  70.4 20.5 %collective-permute-start.16 = (bf16[8,48,896]{2,1,0:T(8,128)(2,1)}, bf16[8,48,896]{2,1,0:T(8,128)(2,1)S(1)}, u32[]{:S(2)}, u32[]{:S(2)}) collective-permute-start(bf16[8,48,896]{2,1,0:T(8,128)(2,1)} %pad_maximum_fusion.4), channel_id=1, source_target_pairs={{0,2},{2,0},{4,6},{6,4},{8,10},{10,8},{12,14},{14,12},{16,18},{18,... | collective-permute-start | bytes 2064392 | tf_op jit(solution)/shard_map/ppermute | solution.py:837
  100.6 15.1 %collective-permute-start.20 = (bf16[512,768]{1,0:T(8,128)(2,1)S(1)}, bf16[512,768]{1,0:T(8,128)(2,1)S(1)}, u32[]{:S(2)}, u32[]{:S(2)}) collective-permute-start(bf16[512,768]{1,0:T(8,128)(2,1)S(1)} %bitcast_select_fusion.n_ref.ng_ref.c_ref), channel_id=1, source_target_pairs={{0,1},{1,0},{2,3},{3,2},{4,5},{5,4},{6,7},{7,6},{8,9},{9,8},{10,11... | collective-permute-start | bytes 2359304 | tf_op jit(solution)/shard_map/ppermute | solution.py:833
  131.2 104.3 %reduce-scatter.5.cloned.1.call-start = ((), (), s32[]{:S(2)}) async-start(), calls=%async_computation.4 | async-start | bytes 737280 | tf_op jit(solution)/shard_map/reduce_scatter | solution.py:993
  132.3 23.7 %collective-permute-start.21 = (bf16[512,768]{1,0:T(8,128)(2,1)S(1)}, bf16[512,768]{1,0:T(8,128)(2,1)S(1)}, u32[]{:S(2)}, u32[]{:S(2)}) collective-permute-start(bf16[512,768]{1,0:T(8,128)(2,1)S(1)} %copy-done.40), channel_id=1, source_target_pairs={{0,1},{1,0},{2,3},{3,2},{4,5},{5,4},{6,7},{7,6},{8,9},{9,8},{10,11... | collective-permute-start | bytes 2359304 | tf_op jit(solution)/shard_map/ppermute | solution.py:833
  154.1 22.8 %collective-permute-start.24 = (bf16[400,768]{1,0:T(8,128)(2,1)}, bf16[400,768]{1,0:T(8,128)(2,1)S(1)}, u32[]{:S(2)}, u32[]{:S(2)}) collective-permute-start(bf16[400,768]{1,0:T(8,128)(2,1)} %get-tuple-element.155), channel_id=1, source_target_pairs={{0,2},{2,0},{4,6},{6,4},{8,10},{10,8},{12,14},{14,12},{16,18},{18,... | collective-permute-start | bytes 1843208 | tf_op jit(solution)/shard_map/ppermute | solution.py:837
  155.4 22.4 %collective-permute-start.25 = (bf16[400,768]{1,0:T(8,128)(2,1)}, bf16[400,768]{1,0:T(8,128)(2,1)S(1)}, u32[]{:S(2)}, u32[]{:S(2)}) collective-permute-start(bf16[400,768]{1,0:T(8,128)(2,1)} %get-tuple-element.156), channel_id=1, source_target_pairs={{0,4},{2,6},{4,0},{6,2},{8,12},{10,14},{12,8},{14,10},{16,20},{18,... | collective-permute-start | bytes 1843208 | tf_op jit(solution)/shard_map/ppermute | solution.py:837
  178.6 10.7 %collective-permute-start.26 = (bf16[512,1536]{1,0:T(8,128)(2,1)}, bf16[512,1536]{1,0:T(8,128)(2,1)S(1)}, u32[]{:S(2)}, u32[]{:S(2)}) collective-permute-start(bf16[512,1536]{1,0:T(8,128)(2,1)} %get-tuple-element.159), channel_id=1, source_target_pairs={{1,0},{3,2},{5,4},{7,6},{9,8},{11,10},{13,12},{15,14},{17,16},{19,... | collective-permute-start | bytes 4718600 | tf_op jit(solution)/shard_map/ppermute | solution.py:992
  196.4 12.8 %collective-permute-start.29 = (bf16[8,24,3072]{2,1,0:T(8,128)(2,1)S(1)}, bf16[8,24,3072]{2,1,0:T(8,128)(2,1)}, u32[]{:S(2)}, u32[]{:S(2)}) collective-permute-start(bf16[8,24,3072]{2,1,0:T(8,128)(2,1)S(1)} %get-tuple-element.176), channel_id=1, source_target_pairs={{0,1},{1,0},{2,3},{3,2},{4,5},{5,4},{6,7},{7,6},{8,9},{9,8},{10,11... | collective-permute-start | bytes 3538952 | tf_op jit(solution)/shard_map/ppermute | solution.py:833
  198.5 10.7 %collective-permute-start.27 = (bf16[8,24,1536]{2,1,0:T(8,128)(2,1)}, bf16[8,24,1536]{2,1,0:T(8,128)(2,1)}, u32[]{:S(2)}, u32[]{:S(2)}) collective-permute-start(bf16[8,24,1536]{2,1,0:T(8,128)(2,1)} %get-tuple-element.174), channel_id=1, source_target_pairs={{0,1},{1,0},{2,3},{3,2},{4,5},{5,4},{6,7},{7,6},{8,9},{9,8},{10,11... | collective-permute-start | bytes 1769480 | tf_op jit(solution)/shard_map/ppermute | solution.py:833
  215.4 14.1 %collective-permute-start.32 = (bf16[8,24,1536]{2,1,0:T(8,128)(2,1)S(1)}, bf16[8,24,1536]{2,1,0:T(8,128)(2,1)S(1)}, u32[]{:S(2)}, u32[]{:S(2)}) collective-permute-start(bf16[8,24,1536]{2,1,0:T(8,128)(2,1)S(1)} %add_convert_fusion.4), channel_id=1, source_target_pairs={{0,2},{2,0},{4,6},{6,4},{8,10},{10,8},{12,14},{14,12},{16,18},{18,... | collective-permute-start | bytes 1769480 | tf_op jit(solution)/shard_map/ppermute | solution.py:837
  216.2 14.1 %collective-permute-start.33 = (bf16[8,24,1536]{2,1,0:T(8,128)(2,1)S(1)}, bf16[8,24,1536]{2,1,0:T(8,128)(2,1)S(1)}, u32[]{:S(2)}, u32[]{:S(2)}) collective-permute-start(bf16[8,24,1536]{2,1,0:T(8,128)(2,1)S(1)} %add_convert_fusion.3), channel_id=1, source_target_pairs={{0,4},{2,6},{4,0},{6,2},{8,12},{10,14},{12,8},{14,10},{16,20},{18,... | collective-permute-start | bytes 1769480 | tf_op jit(solution)/shard_map/ppermute | solution.py:837
  219.4 24.7 %collective-permute-start.37 = (bf16[64,1536]{1,0:T(8,128)(2,1)}, bf16[64,1536]{1,0:T(8,128)(2,1)}, u32[]{:S(2)}, u32[]{:S(2)}) collective-permute-start(bf16[64,1536]{1,0:T(8,128)(2,1)} %get-tuple-element.200), channel_id=1, source_target_pairs={{0,8},{2,10},{4,12},{6,14},{8,0},{10,2},{12,4},{14,6},{16,24},{18,... | collective-permute-start | bytes 589832 | tf_op jit(solution)/shard_map/ppermute | solution.py:837
  222.0 23.9 %collective-permute-start.38 = (bf16[64,1536]{1,0:T(8,128)(2,1)}, bf16[64,1536]{1,0:T(8,128)(2,1)}, u32[]{:S(2)}, u32[]{:S(2)}) collective-permute-start(bf16[64,1536]{1,0:T(8,128)(2,1)} %get-tuple-element.201), channel_id=1, source_target_pairs={{0,16},{2,18},{4,20},{6,22},{8,24},{10,26},{12,28},{14,30},{16,0},... | collective-permute-start | bytes 589832 | tf_op jit(solution)/shard_map/ppermute | solution.py:837
  222.3 23.6 %collective-permute-start.39 = (bf16[64,1536]{1,0:T(8,128)(2,1)}, bf16[64,1536]{1,0:T(8,128)(2,1)}, u32[]{:S(2)}, u32[]{:S(2)}) collective-permute-start(bf16[64,1536]{1,0:T(8,128)(2,1)} %get-tuple-element.202), channel_id=1, source_target_pairs={{0,24},{2,26},{4,28},{6,30},{8,16},{10,18},{12,20},{14,22},{16,8},... | collective-permute-start | bytes 589832 | tf_op jit(solution)/shard_map/ppermute | solution.py:837
  242.7 10.8 %collective-permute-start.40 = (bf16[24,3072]{1,0:T(8,128)(2,1)S(1)}, bf16[24,3072]{1,0:T(8,128)(2,1)S(1)}, u32[]{:S(2)}, u32[]{:S(2)}) collective-permute-start(bf16[24,3072]{1,0:T(8,128)(2,1)S(1)} %get-tuple-element.204), channel_id=1, source_target_pairs={{0,16},{2,18},{4,20},{6,22},{8,24},{10,26},{12,28},{14,30},{16,0},... | collective-permute-start | bytes 442376 | tf_op jit(solution)/shard_map/ppermute | solution.py:837
  (63 other events, 434.2 us)
Sparse Core Ops, SparseCore 0:
  39.1 64.5 all-gather.1
  131.3 43.9 reduce-scatter.2
  201.2 22.1 reduce-scatter.4

commit v3 on v2

--- a/solution.py
+++ b/solution.py
@@ -13,7 +13,7 @@
 F32 = jnp.float32
 BF16 = jnp.bfloat16
 VMEM_LIMIT = 60 * 1024 * 1024
-VMEM_LIMITS = {"project_grads": 30 * 1024 * 1024, "finish": 30 * 1024 * 1024}
+VMEM_LIMITS = {"project_grads": 30 * 1024 * 1024, "project_back": 30 * 1024 * 1024, "finish": 30 * 1024 * 1024}
 TILE = 256
 EXTRA = 16
 COST_SCALE = 0.05

time: 263 us -> 263 us (level)
  waiting for transfers between devices: 63.5 us -> 67.6 us
  other arithmetic: 21.9 us -> 19 us
    unnamed x82 -> x102, local copies, waits for them, and re-layouts: 9.88 us -> 13.4 us
    pallas_call x1, Pallas kernels: 7.07 us -> 4.1 us  [project_back(): call(body, 'project_back', shaped((rows, width), BF16), (rows // tile,),...]
    ppermute x28, waiting for transfers between devices: 51.9 us -> 54.7 us  [exchange(): return lax.ppermute(array, CHIPS, [(i, i ^ mask) for i in range(chips)])]
  transfers between devices with their start and end apart: 46 -> 46, of which waited for: 25 -> 25; matrix products, arithmetic and copies ran while one was open for 9% -> 7% of each run, Pallas kernels for 30% -> 29%
where the time goes in v3:
time: 263 us; the launch traced here: 262 us
  Pallas kernels  97.4 us (37%)
  waiting for transfers between devices  67.6 us (26%)
  starting transfers between devices  46 us (17%)
  other arithmetic  19 us (7%)
  local copies, waits for them, and re-layouts  17 us (6%)
  between operations  15.2 us (6%)
    ppermute x28, waiting for transfers between devices, exchange(): return lax.ppermute(array, CHIPS, [(i, i ^ mask) for i in range(chips)])  54.7 us
    ppermute x28, starting transfers between devices, exchange(): return lax.ppermute(array, CHIPS, [(i, i ^ mask) for i in range(chips)])  38 us
    pallas_call x1, Pallas kernels, ffn_back(): call(body, 'ffn_back', (shaped((rows, width), BF16), shaped((rows, width)...  20.4 us
    pallas_call x1, Pallas kernels, ffn_out(): call(body, 'ffn_out', (shaped((rows, width), BF16), shaped((rows, width),...  14 us
    unnamed x102, local copies, waits for them, and re-layouts  13.4 us
    pallas_call x1, Pallas kernels, attend_back(): call(body, 'attend_back', (shaped((rows, width), BF16), shaped((rows, 2 *...  12 us
    pallas_call x1, Pallas kernels, ffn_in(): call(body, 'ffn_in', (shaped((2 * rows, units), BF16), shaped((2 * rows,...  10.4 us
    pallas_call x1, Pallas kernels, attend(): call(body, 'attend', (shaped((rows, width), BF16), shaped((pairs, 8, rows...  8.67 us
  transfers between devices with their start and end apart: 46, of which 25 were waited for; matrix products, arithmetic and copies ran while one was open for 7% of the time, Pallas kernels for 29%

profile of v3, /device:TPU:0, one launch (start us, length us, event | category | flops | bytes accessed | tf_op | source)
XLA Modules:
  0.0 262.1 jit_solution(9642743736431051273)
XLA Ops:
  9.0 4.1 %collective-permute-start.1 = (bf16[24,2560]{1,0:T(8,128)(2,1)S(1)}, bf16[24,2560]{1,0:T(8,128)(2,1)S(1)}, u32[]{:S(2)}, u32[]{:S(2)}) collective-permute-start(bf16[24,2560]{1,0:T(8,128)(2,1)S(1)} %get-tuple-element.245), channel_id=1, source_target_pairs={{0,16},{2,18},{4,20},{6,22},{8,24},{10,26},{12,28},{14,30},{16,0},... | collective-permute-start | bytes 368648 | tf_op jit(solution)/shard_map/ppermute | solution.py:837
  16.3 4.4 %collective-permute-done.1 = bf16[24,2560]{1,0:T(8,128)(2,1)S(1)} collective-permute-done((bf16[24,2560]{1,0:T(8,128)(2,1)S(1)}, bf16[24,2560]{1,0:T(8,128)(2,1)S(1)}, u32[]{:S(2)}, u32[]{:S(2)}) %collective-permute-start.1) | collective-permute-done | bytes 122912 | tf_op jit(solution)/shard_map/ppermute | solution.py:837
  26.0 3.8 %collective-permute-done.4 = bf16[4,24,1280]{2,1,0:T(8,128)(2,1)S(1)} collective-permute-done((bf16[4,24,1280]{2,1,0:T(8,128)(2,1)S(1)}, bf16[4,24,1280]{2,1,0:T(8,128)(2,1)S(1)}, u32[]{:S(2)}, u32[]{:S(2)}) %collective-permute-start.4) | collective-permute-done | bytes 245792 | tf_op jit(solution)/shard_map/ppermute | solution.py:837
  33.2 2.4 collective-permute-start.9
  35.6 2.8 %collective-permute-start.8 = (bf16[48,1920]{1,0:T(8,128)(2,1)S(1)}, bf16[48,1920]{1,0:T(8,128)(2,1)S(1)}, u32[]{:S(2)}, u32[]{:S(2)}) collective-permute-start(bf16[48,1920]{1,0:T(8,128)(2,1)S(1)} %maximum_maximum_fusion), channel_id=1, source_target_pairs={{0,16},{2,18},{4,20},{6,22},{8,24},{10,26},{12,28},{14,30},{16,0},... | collective-permute-start | bytes 552968 | tf_op jit(solution)/shard_map/ppermute | solution.py:837
  41.3 10.5 %collective-permute-done.8 = bf16[48,1920]{1,0:T(8,128)(2,1)S(1)} collective-permute-done((bf16[48,1920]{1,0:T(8,128)(2,1)S(1)}, bf16[48,1920]{1,0:T(8,128)(2,1)S(1)}, u32[]{:S(2)}, u32[]{:S(2)}) %collective-permute-start.8) | collective-permute-done | bytes 184352 | tf_op jit(solution)/shard_map/ppermute | solution.py:837
  57.2 8.2 %project.1 = (bf16[512,768]{1,0:T(8,128)(2,1)}, bf16[512,1536]{1,0:T(8,128)(2,1)}, bf16[512,768]{1,0:T(8,128)(2,1)}, bf16[768,2304]{1,0:T(8,128)(2,1)}, f32[8,768]{1,0:T(8,128)}) custom-call(s32[8]{0:T(128)} %pad_add_fusion.s_ref, bf16[512,768]{1,0:T(8,128)(2,1)} %bitcast.43, bf16[16,24,1280]{2,1,0:T(8,128)(2,1)} %copy-done.22, ...), custom_call_target="tpu_custom_call" | custom-call | flops 1 | bytes 1476000 | tf_op jit(solution)/shard_map/project/pallas_call | solution.py:154
  72.5 8.7 %attend.1 = (bf16[512,768]{1,0:T(8,128)(2,1)}, f32[6,8,512]{2,1,0:T(8,128)}) custom-call(s32[8]{0:T(128)} %pad_add_fusion.s_ref, bf16[512,768]{1,0:T(8,128)(2,1)} %get-tuple-element.123.q_ref, bf16[512,1536]{1,0:T(8,128)(2,1)} %get-tuple-element.125.kv_ref, bf16[512,1536]{1,0:T(8,128)(2,1)} %copy-done.20), custom_call_target="tpu_custom_call" | custom-call | flops 1 | bytes 2767500 | tf_op jit(solution)/shard_map/attend/pallas_call | solution.py:233
  81.1 9.6 %collective-permute-done.16.refs_5_ = bf16[8,48,896]{2,1,0:T(8,128)(2,1)S(1)} collective-permute-done((bf16[8,48,896]{2,1,0:T(8,128)(2,1)}, bf16[8,48,896]{2,1,0:T(8,128)(2,1)S(1)}, u32[]{:S(2)}, u32[]{:S(2)}) %collective-permute-start.16) | collective-permute-done | bytes 688160 | tf_op jit(solution)/shard_map/ppermute | solution.py:837
  95.2 5.1 %join.1 = (bf16[512,768]{1,0:T(8,128)(2,1)}, f32[512,768]{1,0:T(8,128)}, bf16[512,768]{1,0:T(8,128)(2,1)}, bf16[768,768]{1,0:T(8,128)(2,1)}) custom-call(s32[8]{0:T(128)} %pad_add_fusion.s_ref, bf16[512,768]{1,0:T(8,128)(2,1)} %get-tuple-element.131.a_ref.o_ref, bf16[512,768]{1,0:T(8,128)(2,1)} %bitcast.44, f32[8,768]{1,0:T(8,128)} %get-tuple-element.132.g_ref.refs_4_, ...), custom_call_target="tpu_custom_call" | custom-call | flops 1 | bytes 922500 | tf_op jit(solution)/shard_map/join/pallas_call | solution.py:364
  101.0 2.7 %all-gather.2.cloned.1.call-done = bf16[768,1536]{1,0:T(8,128)(2,1)} async-done(((bf16[48,1536]{1,0:T(8,128)(2,1)}), bf16[768,1536]{1,0:T(8,128)(2,1)}) %all-gather.2.cloned.1.call-update) | async-done | bytes 2359312 | tf_op jit(solution)/shard_map/all_gather | solution.py:905
  104.6 10.4 %ffn_in.1 = (bf16[1024,1536]{1,0:T(8,128)(2,1)}, bf16[1024,1536]{1,0:T(8,128)(2,1)}, f32[8,1024]{1,0:T(8,128)}, bf16[768,1536]{1,0:T(8,128)(2,1)}) custom-call(s32[8]{0:T(128)} %pad_add_fusion.s_ref, bf16[512,768]{1,0:T(8,128)(2,1)} %get-tuple-element.134.n_ref, bf16[512,768]{1,0:T(8,128)(2,1)} %copy-done.25, bf16[4,48,1024]{2,1,0:T(8,128)(2,1)} %copy-done.24, ...), custom_call_target="tpu_custom_call" | custom-call | flops 1 | bytes 1845000 | tf_op jit(solution)/shard_map/ffn_in/pallas_call | solution.py:505
  117.1 14.0 %ffn_out.1 = (bf16[512,768]{1,0:T(8,128)(2,1)}, bf16[512,768]{1,0:T(8,128)(2,1)}, f32[8,1024]{1,0:T(8,128)}, bf16[768,1536]{1,0:T(8,128)(2,1)}) custom-call(s32[8]{0:T(128)} %pad_add_fusion.s_ref, bf16[1024,1536]{1,0:T(8,128)(2,1)} %get-tuple-element.137.a_ref, f32[8,1024]{1,0:T(8,128)} %get-tuple-element.138.st_ref, f32[8,1024]{1,0:T(8,128)} %copy-done.40, ...), custom_call_target="tpu_custom_call" | custom-call | flops 1 | bytes 1845000 | tf_op jit(solution)/shard_map/ffn_out/pallas_call | solution.py:560
  133.7 20.4 %ffn_back.1 = (bf16[512,768]{1,0:T(8,128)(2,1)}, bf16[512,768]{1,0:T(8,128)(2,1)}, f32[8,1536]{1,0:T(8,128)}, bf16[384,1536]{1,0:T(8,128)(2,1)}, bf16[400,768]{1,0:T(8,128)(2,1)}, /*index=5*/bf16[400,768]{1,0:T(8,128)(2,1)}) custom-call(s32[8]{0:T(128)} %pad_add_fusion.s_ref, bf16[1024,1536]{1,0:T(8,128)(2,1)} %get-tuple-element.137.a_ref, ...), custom_call_target="tpu_custom_call" | custom-call | flops 1 | bytes 2583000 | tf_op jit(solution)/shard_map/ffn_back/pallas_call | solution.py:659
  157.6 7.3 %join_back.1 = (bf16[512,768]{1,0:T(8,128)(2,1)}, f32[512,768]{1,0:T(8,128)}, bf16[512,768]{1,0:T(8,128)(2,1)}, bf16[512,768]{1,0:T(8,128)(2,1)}) custom-call(s32[8]{0:T(128)} %pad_add_fusion.s_ref, bf16[512,768]{1,0:T(8,128)(2,1)} %get-tuple-element.140.b_ref, bf16[512,768]{1,0:T(8,128)(2,1)} %copy-done.34, bf16[512,768]{1,0:T(8,128)(2,1)} %get-tuple-element.145.f_ref, ...), custom_call_target="tpu_custom_call" | custom-call | flops 1 | bytes 1291500 | tf_op jit(solution)/shard_map/join_back/pallas_call | solution.py:405
  164.9 12.0 %attend_back.1 = (bf16[512,768]{1,0:T(8,128)(2,1)}, bf16[512,1536]{1,0:T(8,128)(2,1)}, bf16[512,1536]{1,0:T(8,128)(2,1)}) custom-call(s32[8]{0:T(128)} %pad_add_fusion.s_ref, bf16[512,768]{1,0:T(8,128)(2,1)} %get-tuple-element.123.q_ref, bf16[512,1536]{1,0:T(8,128)(2,1)} %get-tuple-element.125.kv_ref, bf16[512,1536]{1,0:T(8,128)(2,1)} %copy-done.20, ...), custom_call_target="tpu_custom_call" | custom-call | flops 1 | bytes 3690000 | tf_op jit(solution)/shard_map/attend_back/pallas_call | solution.py:330
  184.2 5.1 %collective-permute-done.26.fkv_ref = bf16[512,1536]{1,0:T(8,128)(2,1)S(1)} collective-permute-done((bf16[512,1536]{1,0:T(8,128)(2,1)}, bf16[512,1536]{1,0:T(8,128)(2,1)S(1)}, u32[]{:S(2)}, u32[]{:S(2)}) %collective-permute-start.26) | collective-permute-done | bytes 1572896 | tf_op jit(solution)/shard_map/ppermute | solution.py:992
  189.4 6.0 %project_grads.1 = (bf16[512,2304]{1,0:T(8,128)(2,1)S(1)}, bf16[8,24,3072]{2,1,0:T(8,128)(2,1)S(1)}, bf16[8,24,1536]{2,1,0:T(8,128)(2,1)S(1)}, bf16[8,24,1536]{2...) custom-call(s32[8]{0:T(128)S(1)} %copy-done.18, ...), custom_call_target="tpu_custom_call" | custom-call | flops 1 | bytes 2029500 | tf_op jit(solution)/shard_map/project_grads/pallas_call | solution.py:744
  205.6 4.1 %project_back.1 = bf16[512,768]{1,0:T(8,128)(2,1)} custom-call(s32[8]{0:T(128)S(1)} %copy-done.18, bf16[512,2304]{1,0:T(8,128)(2,1)S(1)} %get-tuple-element.167.refs_0_, bf16[512,768]{1,0:T(8,128)(2,1)S(1)} %bitcast.45, f32[512,768]{1,0:T(8,128)S(1)} %copy-done.3, bf16[768,2304]{1,0:T(8,128)(2,1)S(1)} %copy-done.1, f32[8,768]{1,0:T(8,128)S(1)} %copy-done.15), custom_call_target="tpu_custom_call" | custom-call | flops 1 | bytes 1291500 | tf_op jit(solution)/shard_map/project_back/pallas_call | solution.py:817
  217.5 2.5 collective-permute-start.37
  222.5 6.7 %collective-permute-done.32 = bf16[8,24,1536]{2,1,0:T(8,128)(2,1)S(1)} collective-permute-done((bf16[8,24,1536]{2,1,0:T(8,128)(2,1)S(1)}, bf16[8,24,1536]{2,1,0:T(8,128)(2,1)S(1)}, u32[]{:S(2)}, u32[]{:S(2)}) %collective-permute-start.32) | collective-permute-done | bytes 589856 | tf_op jit(solution)/shard_map/ppermute | solution.py:837
  235.5 3.4 %collective-permute-done.34 = bf16[4,24,1536]{2,1,0:T(8,128)(2,1)S(1)} collective-permute-done((bf16[4,24,1536]{2,1,0:T(8,128)(2,1)S(1)}, bf16[4,24,1536]{2,1,0:T(8,128)(2,1)S(1)}, u32[]{:S(2)}, u32[]{:S(2)}) %collective-permute-start.34) | collective-permute-done | bytes 294944 | tf_op jit(solution)/shard_map/ppermute | solution.py:837
  245.5 2.7 %collective-permute-done.36.refs_1_ = bf16[24,3072]{1,0:T(8,128)(2,1)S(1)} collective-permute-done((bf16[24,3072]{1,0:T(8,128)(2,1)S(1)}, bf16[24,3072]{1,0:T(8,128)(2,1)S(1)}, u32[]{:S(2)}, u32[]{:S(2)}) %collective-permute-start.36) | collective-permute-done | bytes 147488 | tf_op jit(solution)/shard_map/ppermute | solution.py:837
  250.4 3.2 %collective-permute-done.40.refs_2_ = bf16[24,3072]{1,0:T(8,128)(2,1)S(1)} collective-permute-done((bf16[24,3072]{1,0:T(8,128)(2,1)S(1)}, bf16[24,3072]{1,0:T(8,128)(2,1)S(1)}, u32[]{:S(2)}, u32[]{:S(2)}) %collective-permute-start.40) | collective-permute-done | bytes 147488 | tf_op jit(solution)/shard_map/ppermute | solution.py:837
  (245 shorter events, 87.1 us)
Async XLA Ops:
  7.2 96.5 %all-gather.2.cloned.1.call-start = ((), (), s32[]{:S(2)}) async-start(), calls=%async_computation.2 | async-start | bytes 2506752 | tf_op jit(solution)/shard_map/all_gather | solution.py:905
  9.0 11.7 %collective-permute-start.1 = (bf16[24,2560]{1,0:T(8,128)(2,1)S(1)}, bf16[24,2560]{1,0:T(8,128)(2,1)S(1)}, u32[]{:S(2)}, u32[]{:S(2)}) collective-permute-start(bf16[24,2560]{1,0:T(8,128)(2,1)S(1)} %get-tuple-element.245), channel_id=1, source_target_pairs={{0,16},{2,18},{4,20},{6,22},{8,24},{10,26},{12,28},{14,30},{16,0},... | collective-permute-start | bytes 368648 | tf_op jit(solution)/shard_map/ppermute | solution.py:837
  31.1 21.7 %collective-permute-start.6 = (bf16[8,24,1280]{2,1,0:T(8,128)(2,1)S(1)}, bf16[8,24,1280]{2,1,0:T(8,128)(2,1)S(1)}, u32[]{:S(2)}, u32[]{:S(2)}) collective-permute-start(bf16[8,24,1280]{2,1,0:T(8,128)(2,1)S(1)} %pad_maximum_fusion.9), channel_id=1, source_target_pairs={{0,4},{2,6},{4,0},{6,2},{8,12},{10,14},{12,8},{14,10},{16,20},{18,... | collective-permute-start | bytes 1474568 | tf_op jit(solution)/shard_map/ppermute | solution.py:837
  32.7 20.1 %collective-permute-start.5 = (bf16[8,24,1280]{2,1,0:T(8,128)(2,1)S(1)}, bf16[8,24,1280]{2,1,0:T(8,128)(2,1)S(1)}, u32[]{:S(2)}, u32[]{:S(2)}) collective-permute-start(bf16[8,24,1280]{2,1,0:T(8,128)(2,1)S(1)} %pad_maximum_fusion.8), channel_id=1, source_target_pairs={{0,2},{2,0},{4,6},{6,4},{8,10},{10,8},{12,14},{14,12},{16,18},{18,... | collective-permute-start | bytes 1474568 | tf_op jit(solution)/shard_map/ppermute | solution.py:837
  35.6 16.1 %collective-permute-start.8 = (bf16[48,1920]{1,0:T(8,128)(2,1)S(1)}, bf16[48,1920]{1,0:T(8,128)(2,1)S(1)}, u32[]{:S(2)}, u32[]{:S(2)}) collective-permute-start(bf16[48,1920]{1,0:T(8,128)(2,1)S(1)} %maximum_maximum_fusion), channel_id=1, source_target_pairs={{0,16},{2,18},{4,20},{6,22},{8,24},{10,26},{12,28},{14,30},{16,0},... | collective-permute-start | bytes 552968 | tf_op jit(solution)/shard_map/ppermute | solution.py:837
  38.4 13.3 %collective-permute-start.7 = (bf16[48,1920]{1,0:T(8,128)(2,1)S(1)}, bf16[48,1920]{1,0:T(8,128)(2,1)}, u32[]{:S(2)}, u32[]{:S(2)}) collective-permute-start(bf16[48,1920]{1,0:T(8,128)(2,1)S(1)} %maximum_maximum_fusion), channel_id=1, source_target_pairs={{0,8},{2,10},{4,12},{6,14},{8,0},{10,2},{12,4},{14,6},{16,24},{18,... | collective-permute-start | bytes 552968 | tf_op jit(solution)/shard_map/ppermute | solution.py:837
  39.0 138.8 %reduce-scatter.3.cloned.1.call-start = ((), (), s32[]{:S(2)}) async-start(), calls=%async_computation.3 | async-start | bytes 2949120 | tf_op jit(solution)/shard_map/reduce_scatter | solution.py:966
  53.9 11.6 %collective-permute-start.12 = (bf16[4,48,1024]{2,1,0:T(8,128)(2,1)S(1)}, bf16[4,48,1024]{2,1,0:T(8,128)(2,1)S(1)}, u32[]{:S(2)}, u32[]{:S(2)}) collective-permute-start(bf16[4,48,1024]{2,1,0:T(8,128)(2,1)S(1)} %slice.185.refs_0_), channel_id=1, source_target_pairs={{0,2},{2,0},{4,6},{6,4},{8,10},{10,8},{12,14},{14,12},{16,18},{18,... | collective-permute-start | bytes 1179656 | tf_op jit(solution)/shard_map/ppermute | solution.py:837
  68.7 23.5 %collective-permute-start.15 = (bf16[8,48,1024]{2,1,0:T(8,128)(2,1)}, bf16[8,48,1024]{2,1,0:T(8,128)(2,1)}, u32[]{:S(2)}, u32[]{:S(2)}) collective-permute-start(bf16[8,48,1024]{2,1,0:T(8,128)(2,1)} %pad_maximum_fusion.2), channel_id=1, source_target_pairs={{0,4},{2,6},{4,0},{6,2},{8,12},{10,14},{12,8},{14,10},{16,20},{18,... | collective-permute-start | bytes 2359304 | tf_op jit(solution)/shard_map/ppermute | solution.py:837
  70.3 20.4 %collective-permute-start.16 = (bf16[8,48,896]{2,1,0:T(8,128)(2,1)}, bf16[8,48,896]{2,1,0:T(8,128)(2,1)S(1)}, u32[]{:S(2)}, u32[]{:S(2)}) collective-permute-start(bf16[8,48,896]{2,1,0:T(8,128)(2,1)} %pad_maximum_fusion.4), channel_id=1, source_target_pairs={{0,2},{2,0},{4,6},{6,4},{8,10},{10,8},{12,14},{14,12},{16,18},{18,... | collective-permute-start | bytes 2064392 | tf_op jit(solution)/shard_map/ppermute | solution.py:837
  100.6 15.2 %collective-permute-start.20 = (bf16[512,768]{1,0:T(8,128)(2,1)S(1)}, bf16[512,768]{1,0:T(8,128)(2,1)S(1)}, u32[]{:S(2)}, u32[]{:S(2)}) collective-permute-start(bf16[512,768]{1,0:T(8,128)(2,1)S(1)} %bitcast_select_fusion.n_ref.ng_ref.c_ref), channel_id=1, source_target_pairs={{0,1},{1,0},{2,3},{3,2},{4,5},{5,4},{6,7},{7,6},{8,9},{9,8},{10,11... | collective-permute-start | bytes 2359304 | tf_op jit(solution)/shard_map/ppermute | solution.py:833
  131.2 104.3 %reduce-scatter.5.cloned.1.call-start = ((), (), s32[]{:S(2)}) async-start(), calls=%async_computation.4 | async-start | bytes 737280 | tf_op jit(solution)/shard_map/reduce_scatter | solution.py:993
  132.3 23.7 %collective-permute-start.21 = (bf16[512,768]{1,0:T(8,128)(2,1)S(1)}, bf16[512,768]{1,0:T(8,128)(2,1)S(1)}, u32[]{:S(2)}, u32[]{:S(2)}) collective-permute-start(bf16[512,768]{1,0:T(8,128)(2,1)S(1)} %copy-done.50), channel_id=1, source_target_pairs={{0,1},{1,0},{2,3},{3,2},{4,5},{5,4},{6,7},{7,6},{8,9},{9,8},{10,11... | collective-permute-start | bytes 2359304 | tf_op jit(solution)/shard_map/ppermute | solution.py:833
  154.2 22.8 %collective-permute-start.24 = (bf16[400,768]{1,0:T(8,128)(2,1)}, bf16[400,768]{1,0:T(8,128)(2,1)S(1)}, u32[]{:S(2)}, u32[]{:S(2)}) collective-permute-start(bf16[400,768]{1,0:T(8,128)(2,1)} %get-tuple-element.155), channel_id=1, source_target_pairs={{0,2},{2,0},{4,6},{6,4},{8,10},{10,8},{12,14},{14,12},{16,18},{18,... | collective-permute-start | bytes 1843208 | tf_op jit(solution)/shard_map/ppermute | solution.py:837
  155.4 22.4 %collective-permute-start.25 = (bf16[400,768]{1,0:T(8,128)(2,1)}, bf16[400,768]{1,0:T(8,128)(2,1)S(1)}, u32[]{:S(2)}, u32[]{:S(2)}) collective-permute-start(bf16[400,768]{1,0:T(8,128)(2,1)} %get-tuple-element.156), channel_id=1, source_target_pairs={{0,4},{2,6},{4,0},{6,2},{8,12},{10,14},{12,8},{14,10},{16,20},{18,... | collective-permute-start | bytes 1843208 | tf_op jit(solution)/shard_map/ppermute | solution.py:837
  198.1 12.3 %collective-permute-start.29 = (bf16[8,24,3072]{2,1,0:T(8,128)(2,1)}, bf16[8,24,3072]{2,1,0:T(8,128)(2,1)}, u32[]{:S(2)}, u32[]{:S(2)}) collective-permute-start(bf16[8,24,3072]{2,1,0:T(8,128)(2,1)} %get-tuple-element.176), channel_id=1, source_target_pairs={{0,1},{1,0},{2,3},{3,2},{4,5},{5,4},{6,7},{7,6},{8,9},{9,8},{10,11... | collective-permute-start | bytes 3538952 | tf_op jit(solution)/shard_map/ppermute | solution.py:833
  199.6 10.7 %collective-permute-start.27 = (bf16[8,24,1536]{2,1,0:T(8,128)(2,1)}, bf16[8,24,1536]{2,1,0:T(8,128)(2,1)}, u32[]{:S(2)}, u32[]{:S(2)}) collective-permute-start(bf16[8,24,1536]{2,1,0:T(8,128)(2,1)} %get-tuple-element.174), channel_id=1, source_target_pairs={{0,1},{1,0},{2,3},{3,2},{4,5},{5,4},{6,7},{7,6},{8,9},{9,8},{10,11... | collective-permute-start | bytes 1769480 | tf_op jit(solution)/shard_map/ppermute | solution.py:833
  199.6 10.7 %collective-permute-start.28 = (bf16[8,24,1536]{2,1,0:T(8,128)(2,1)}, bf16[8,24,1536]{2,1,0:T(8,128)(2,1)}, u32[]{:S(2)}, u32[]{:S(2)}) collective-permute-start(bf16[8,24,1536]{2,1,0:T(8,128)(2,1)} %get-tuple-element.175), channel_id=1, source_target_pairs={{0,1},{1,0},{2,3},{3,2},{4,5},{5,4},{6,7},{7,6},{8,9},{9,8},{10,11... | collective-permute-start | bytes 1769480 | tf_op jit(solution)/shard_map/ppermute | solution.py:833
  214.9 14.3 %collective-permute-start.32 = (bf16[8,24,1536]{2,1,0:T(8,128)(2,1)S(1)}, bf16[8,24,1536]{2,1,0:T(8,128)(2,1)S(1)}, u32[]{:S(2)}, u32[]{:S(2)}) collective-permute-start(bf16[8,24,1536]{2,1,0:T(8,128)(2,1)S(1)} %add_convert_fusion.4), channel_id=1, source_target_pairs={{0,2},{2,0},{4,6},{6,4},{8,10},{10,8},{12,14},{14,12},{16,18},{18,... | collective-permute-start | bytes 1769480 | tf_op jit(solution)/shard_map/ppermute | solution.py:837
  215.9 14.4 %collective-permute-start.33 = (bf16[8,24,1536]{2,1,0:T(8,128)(2,1)S(1)}, bf16[8,24,1536]{2,1,0:T(8,128)(2,1)S(1)}, u32[]{:S(2)}, u32[]{:S(2)}) collective-permute-start(bf16[8,24,1536]{2,1,0:T(8,128)(2,1)S(1)} %add_convert_fusion.3), channel_id=1, source_target_pairs={{0,4},{2,6},{4,0},{6,2},{8,12},{10,14},{12,8},{14,10},{16,20},{18,... | collective-permute-start | bytes 1769480 | tf_op jit(solution)/shard_map/ppermute | solution.py:837
  217.5 26.8 %collective-permute-start.37 = (bf16[64,1536]{1,0:T(8,128)(2,1)S(1)}, bf16[64,1536]{1,0:T(8,128)(2,1)S(1)}, u32[]{:S(2)}, u32[]{:S(2)}) collective-permute-start(bf16[64,1536]{1,0:T(8,128)(2,1)S(1)} %get-tuple-element.200), channel_id=1, source_target_pairs={{0,8},{2,10},{4,12},{6,14},{8,0},{10,2},{12,4},{14,6},{16,24},{18,... | collective-permute-start | bytes 589832 | tf_op jit(solution)/shard_map/ppermute | solution.py:837
  220.1 25.4 %collective-permute-start.38 = (bf16[64,1536]{1,0:T(8,128)(2,1)S(1)}, bf16[64,1536]{1,0:T(8,128)(2,1)S(1)}, u32[]{:S(2)}, u32[]{:S(2)}) collective-permute-start(bf16[64,1536]{1,0:T(8,128)(2,1)S(1)} %get-tuple-element.201), channel_id=1, source_target_pairs={{0,16},{2,18},{4,20},{6,22},{8,24},{10,26},{12,28},{14,30},{16,0},... | collective-permute-start | bytes 589832 | tf_op jit(solution)/shard_map/ppermute | solution.py:837
  220.8 24.7 %collective-permute-start.39 = (bf16[64,1536]{1,0:T(8,128)(2,1)S(1)}, bf16[64,1536]{1,0:T(8,128)(2,1)S(1)}, u32[]{:S(2)}, u32[]{:S(2)}) collective-permute-start(bf16[64,1536]{1,0:T(8,128)(2,1)S(1)} %get-tuple-element.202), channel_id=1, source_target_pairs={{0,24},{2,26},{4,28},{6,30},{8,16},{10,18},{12,20},{14,22},{16,8},... | collective-permute-start | bytes 589832 | tf_op jit(solution)/shard_map/ppermute | solution.py:837
  242.3 11.3 %collective-permute-start.40 = (bf16[24,3072]{1,0:T(8,128)(2,1)S(1)}, bf16[24,3072]{1,0:T(8,128)(2,1)S(1)}, u32[]{:S(2)}, u32[]{:S(2)}) collective-permute-start(bf16[24,3072]{1,0:T(8,128)(2,1)S(1)} %get-tuple-element.204), channel_id=1, source_target_pairs={{0,16},{2,18},{4,20},{6,22},{8,24},{10,26},{12,28},{14,30},{16,0},... | collective-permute-start | bytes 442376 | tf_op jit(solution)/shard_map/ppermute | solution.py:837
  (75 other events, 505.5 us)
Sparse Core Ops, SparseCore 0:
  39.1 64.5 all-gather.1
  131.3 43.9 reduce-scatter.2
  202.3 23.2 reduce-scatter.4
